TPU v7x, 32 devices: a whole 2x2x4 slice. The times are simulated.
32 devices in a mesh: groups: 2 (over y), rows: 4 (over z), section: 2 (over x), feat: 2 (over core).
Axes of the slice: x: 2, y: 2, z: 4, core: 2. Of those that a mesh axis runs over, the one named last changes fastest.
Arguments:
- test_rows: bfloat16 [3, 256, 8, 512], P(None, ('groups', 'rows'), 'feat'), parts along dimension 1, may hold values from -6 to 6
- train_cache: bfloat16 [2, 2, 32, 8, 512], P('section', None, ('groups', 'rows'), 'feat'), parts along dimension 2, may hold values from -6 to 6
- pattern: int32 [8, 8], replicated, may hold values 0 or 1
- feat_qkv: bfloat16 [2, 512, 1536], P('section'), may hold values from -0.25 to 0.25
- feat_out: bfloat16 [2, 512, 512], P('section'), may hold values from -0.25 to 0.25
- item_query: bfloat16 [2, 512, 512], P('section'), may hold values from -0.25 to 0.25
- item_out: bfloat16 [2, 512, 512], P('section'), may hold values from -0.25 to 0.25
- gains: float32 [2, 2, 512], P('section'), may hold values from 0.5 to 1.5
Outputs:
- hidden: bfloat16 [2, 3, 256, 8, 512], P('section', None, ('groups', 'rows'), 'feat'), parts along dimension 2
There are 2 independent parts, one for each index of `groups`. A program takes and returns all parts, laid end to end along the dimension named above; an argument that names none is the same for every part. Nothing has to cross between parts.
All inputs are finite; a program needn't handle non-finite values.
Results may differ from a plain program's by a relative error of at most 0.02.
Values may be sent and summed in bfloat16 or wider, within the bound.
No kernel may reach another device: no remote copies, remote signals or barrier semaphores. Data moves between devices by JAX's collectives and lax.ppermute only.
A program may use at most 64 MiB of HBM per device.

v0:
```python
import jax
import jax.numpy as jnp
from jax import lax
from jax.sharding import PartitionSpec as P

HEADS = 8


HIGH = lax.Precision.HIGHEST


def from_behind(block, axis, distance):
    devices = range(lax.axis_size(axis))
    route = [(i - distance, i) for i in devices if i - distance in devices]
    return lax.ppermute(block, axis, route)


def normed(x, gain):
    mean_sq = jnp.mean(x * x, axis=-1, keepdims=True)
    return x * lax.rsqrt(mean_sq + 1e-06) * gain


def per_device(test_rows, train_cache, pattern, feat_qkv, feat_out, item_query, item_out, gains):
    micro, test_n, group_dev, width = test_rows.shape
    heads = HEADS
    head_dim = width // heads
    scale = 1.0 / head_dim**0.5
    section = lax.axis_index("section")
    sections = lax.axis_size("section")
    feat_index = lax.axis_index("feat")
    groups = group_dev * lax.axis_size("feat")
    wqkv = feat_qkv[0]
    wout = feat_out[0]
    wquery = item_query[0]
    witem = item_out[0]
    gain_a = gains[0, 0]
    gain_b = gains[0, 1]
    mine = feat_index * group_dev + jnp.arange(group_dev)
    every = jnp.arange(groups)
    pattern_rows = lax.dynamic_slice_in_dim(pattern, feat_index * group_dev, group_dev, 0)
    allowed = (pattern_rows != 0) | (mine[:, None] == every[None, :])
    cache = train_cache[0]
    buffer = jnp.zeros((micro, test_n, group_dev, width), jnp.bfloat16)
    passed = jnp.zeros((test_n, group_dev, width), jnp.bfloat16)
    ticks = micro + sections - 1
    for tick in range(ticks):
        entering = test_rows[min(tick, micro - 1)]
        current = jnp.where(section == 0, entering, passed).astype(jnp.float32)
        a_local = normed(current, gain_a).astype(jnp.bfloat16)
        flat = a_local.reshape(test_n * group_dev, width)
        qkv = jnp.dot(flat, wqkv, preferred_element_type=jnp.float32).astype(jnp.bfloat16)
        qkv = qkv.reshape(test_n, group_dev, 3 * width)
        query = qkv[:, :, :width]
        pairs = lax.all_gather(qkv[:, :, width:], "feat", axis=1, tiled=True)
        query = query.reshape(test_n, group_dev, heads, head_dim)
        keys = pairs[:, :, :width].reshape(test_n, groups, heads, head_dim)
        values = pairs[:, :, width:].reshape(test_n, groups, heads, head_dim)
        scores = (
            jnp.einsum("rihd,rjhd->rhij", query, keys, preferred_element_type=jnp.float32) * scale
        )
        scores = jnp.where(allowed[None, None], scores, -1e30)
        weights = jax.nn.softmax(scores, axis=-1).astype(jnp.bfloat16)
        mixed = jnp.einsum(
            "rhij,rjhd->rihd", weights, values, preferred_element_type=jnp.float32
        ).astype(jnp.bfloat16)
        feature_term = jnp.dot(
            mixed.reshape(test_n * group_dev, width), wout, preferred_element_type=jnp.float32
        )
        h1 = current + feature_term.reshape(test_n, group_dev, width)
        b_local = normed(h1, gain_b).astype(jnp.bfloat16).reshape(test_n * group_dev, width)
        item_q = jnp.dot(b_local, wquery, preferred_element_type=jnp.float32).astype(jnp.bfloat16)
        item_q = item_q.reshape(test_n, group_dev, heads, head_dim)
        start_top = jnp.full((test_n, group_dev, heads), -1e30, jnp.float32)
        piece = lax.all_gather(cache, "rows", axis=1, tiled=True)
        top = start_top
        count = piece.shape[1]
        piece_k = piece[0].reshape(count, group_dev, heads, head_dim)
        piece_v = piece[1].astype(jnp.float32).reshape(count, group_dev, heads, head_dim)
        item_s = (
            jnp.einsum("rghd,nghd->rghn", item_q, piece_k, preferred_element_type=jnp.float32)
            * scale
        )
        new_top = jnp.maximum(top, jnp.max(item_s, axis=-1))
        expo = jnp.exp(item_s - new_top[..., None])
        total = jnp.sum(expo, axis=-1)
        accum = jnp.einsum("rghn,nghd->rghd", expo, piece_v, precision=HIGH)
        top, total, accum = (new_top, total, accum)
        item_mix = accum / total[..., None]
        item_mix = item_mix.astype(jnp.bfloat16).reshape(test_n * group_dev, width)
        term = jnp.dot(item_mix, witem, preferred_element_type=jnp.float32)
        result = (h1 + term.reshape(test_n, group_dev, width)).astype(jnp.bfloat16)
        slot = tick - section
        valid = (slot >= 0) & (slot < micro)
        place = jnp.clip(slot, 0, micro - 1)
        older = lax.dynamic_index_in_dim(buffer, place, 0, keepdims=False)
        buffer = lax.dynamic_update_index_in_dim(buffer, jnp.where(valid, result, older), place, 0)
        if tick + 1 < ticks:
            passed = from_behind(result, "section", 1)
    return buffer[None]


def solution(mesh):
    return jax.shard_map(
        per_device,
        mesh=mesh,
        in_specs=(
            P(None, ("groups", "rows"), "feat", None),
            P("section", None, ("groups", "rows"), "feat", None),
            P(),
            P("section", None, None),
            P("section", None, None),
            P("section", None, None),
            P("section", None, None),
            P("section", None, None),
        ),
        out_specs=P("section", None, ("groups", "rows"), "feat", None),
        check_vma=False,
    )
```

profile of v0, /device:TPU:7, one launch (start us, length us, event | category | flops | bytes accessed | tf_op | source)
XLA Modules:
  0.0 147.0 jit_solution(2902149152831472718)
XLA Ops:
  0.0 2.0 %fusion.112 = (bf16[1,32,4,512]{3,2,1,0:T(4,128)(2,1)}, bf16[1,32,4,512]{3,2,1,0:T(4,128)(2,1)}, bf16[1,32,4,512]{3,2,1,0:T(4,128)(2,1)S(1)}) fusion(bf16[3,32,4,512]{3,2,1,0:T(4,128)(2,1)} %param.8), kind=kLoop, calls=%fused_computation.197 | loop fusion | bytes 786432 | tf_op jit(solution)/shard_map/slice | solution.py:47
  3.9 2.5 %all_gather.18 = bf16[32,8,1024]{2,0,1:T(8,128)(2,1)S(1)} all-gather(bf16[32,4,1024]{2,0,1:T(8,128)(2,1)S(1)} %copy.168), channel_id=1, replica_groups=mesh['groups'=2,'rows'=4,'section'=2,'feat'=2] {'feat'}, dimensions={1}, use_global_device_ids=true | all-gather | bytes 786432 | tf_op jit(solution)/shard_map/all_gather | solution.py:54
  6.9 1.1 reshape.274
  8.1 1.6 %fusion.115 = (f32[32,8,4]{2,1,0:T(8,128)S(1)}, f32[32,8,4,8]{3,2,1,0:T(4,128)}) fusion(bf16[32,8,8,64]{3,2,0,1:T(8,128)(2,1)S(1)} %reshape.275, bf16[32,4,8,64]{3,2,1,0:T(8,128)(2,1)S(1)} %reshape.284, pred[4,8]{1,0:T(4,128)(4,1)S(1)} %fusion.106), kind=kOutput, calls=%fused_computation.200 | convolution fusion | flops 1081351 | bytes 430112 | tf_op jit(solution)/shard_map/sub | solution.py:62
  9.6 1.7 %fusion.28 = bf16[32,4,8,64]{3,1,2,0:T(4,128)(2,1)S(1)} fusion(bf16[32,8,8,64]{3,2,0,1:T(8,128)(2,1)S(1)} %copy-done.11, f32[32,8,4,8]{3,2,1,0:T(4,128)} %get-tuple-element.27, f32[32,8,4]{2,1,0:T(8,128)S(1)} %get-tuple-element.26), kind=kOutput, calls=%fused_computation.44 | convolution fusion | flops 1130496 | bytes 430080 | tf_op jit(solution)/shard_map/rhij,rjhd->rihd/dot_general | solution.py:63
  12.8 10.9 %all-gather = bf16[1,2,16,4,512]{4,3,2,1,0:T(4,128)(2,1)S(1)} all-gather(bf16[1,2,4,4,512]{4,3,2,1,0:T(4,128)(2,1)S(1)} %copy-done.17), channel_id=2, replica_groups=mesh['groups'=2,'rows'=4,'section'=2,'feat'=2] {'rows'}, dimensions={2}, use_global_device_ids=true | all-gather | bytes 163840 | tf_op jit(solution)/shard_map/all_gather | solution.py:74
  24.8 1.7 %reshape.283 = bf16[16,4,8,64]{3,2,1,0:T(8,128)(2,1)} reshape(bf16[1,1,16,4,512]{4,3,2,1,0:T(4,128)(2,1)} %get-tuple-element.22) | data formatting | bytes 131072 | tf_op jit(solution)/shard_map/reshape | solution.py:78
  26.6 1.7 %fusion.27 = bf16[32,4,8,64]{3,0,2,1:T(8,128)(2,1)S(1)} fusion(f32[32,4,8]{0,2,1:T(8,128)S(1)} %fusion.87, f32[32,4,8,16]{0,3,2,1:T(8,128)} %copy-done.9, f32[32,4,8]{0,2,1:T(8,128)S(1)} %broadcast_maximum_fusion.3, bf16[16,4,8,64]{3,2,1,0:T(8,128)(2,1)} %reshape.283), kind=kOutput, calls=%fused_computation.43 | convolution fusion | flops 12730368 | bytes 270336 | tf_op jit(solution)/shard_map/rghn,nghd->rghd/dot_general | solution.py:86
  29.1 1.8 %dot_general.120 = bf16[32,4,512]{2,0,1:T(8,128)(2,1)} reshape(bf16[32,4,8,64]{3,2,0,1:T(8,128)(2,1)} %copy.95) | data formatting | bytes 262144 | tf_op jit(solution)/shard_map/dot_general | solution.py:90
  31.0 1.8 %fusion.36 = bf16[32,4,512]{2,0,1:T(8,128)(2,1)} fusion(f32[32,4,512]{2,0,1:T(8,128)S(1)} %get-tuple-element.29, bf16[32,4,512]{2,0,1:T(8,128)(2,1)} %dot_general.120, bf16[1,512,512]{2,1,0:T(8,128)(2,1)S(1)} %copy-done.3), kind=kOutput, calls=%fused_computation.64 | convolution fusion | flops 67239936 | bytes 1048576 | tf_op jit(solution)/shard_map/dot_general | solution.py:90
  32.8 1.3 collective-permute-start
  35.7 1.6 %constant_dynamic-slice_fusion.2 = bf16[1,32,4,512]{3,2,1,0:T(4,128)(2,1)} fusion(bf16[3,32,4,512]{3,2,1,0:T(4,128)(2,1)} %copy_dynamic-update-slice_fusion.3, s32[]{:T(128)S(6)} %min.14), kind=kLoop, calls=%fused_computation.190 | loop fusion | bytes 262148 | tf_op jit(solution)/shard_map/jit(dynamic_index_in_dim)/dynamic_slice | solution.py:95
  37.3 1.4 collective-permute-done
  38.7 1.0 fusion.66
  40.6 1.1 convolution_convert_fusion.2
  41.7 1.8 %reshape.246 = bf16[32,4,1536]{2,1,0:T(4,128)(2,1)} reshape(bf16[128,1536]{1,0:T(8,128)(2,1)} %convolution_convert_fusion.2) | data formatting | bytes 786432 | tf_op jit(solution)/shard_map/reshape | solution.py:52
  43.6 1.0 slice.107
  44.7 6.2 %all_gather.20 = bf16[32,8,1024]{2,0,1:T(8,128)(2,1)S(1)} all-gather(bf16[32,4,1024]{2,0,1:T(8,128)(2,1)S(1)} %copy.171), channel_id=1, replica_groups=mesh['groups'=2,'rows'=4,'section'=2,'feat'=2] {'feat'}, dimensions={1}, use_global_device_ids=true | all-gather | bytes 786432 | tf_op jit(solution)/shard_map/all_gather | solution.py:54
  51.8 2.1 %reshape.277 = bf16[32,8,8,64]{3,2,0,1:T(8,128)(2,1)} reshape(bf16[32,8,512]{2,0,1:T(8,128)(2,1)} %get-tuple-element.15) | data formatting | bytes 524288 | tf_op jit(solution)/shard_map/reshape | solution.py:56
  53.8 0.9 reshape.285
  54.7 2.1 %reshape.276 = bf16[32,8,8,64]{3,2,0,1:T(8,128)(2,1)} reshape(bf16[32,8,512]{2,0,1:T(8,128)(2,1)} %get-tuple-element.16) | data formatting | bytes 524288 | tf_op jit(solution)/shard_map/reshape | solution.py:57
  56.8 2.7 %fusion.117 = (f32[32,8,4]{2,1,0:T(8,128)S(1)}, f32[32,8,4,8]{3,2,1,0:T(4,128)}) fusion(bf16[32,8,8,64]{3,2,0,1:T(8,128)(2,1)} %reshape.277, bf16[32,4,8,64]{3,2,1,0:T(8,128)(2,1)} %reshape.285, pred[4,8]{1,0:T(4,128)(4,1)S(1)} %copy-done.20), kind=kOutput, calls=%fused_computation.202 | convolution fusion | flops 1081351 | bytes 430112 | tf_op jit(solution)/shard_map/sub | solution.py:62
  59.5 1.8 %fusion.29 = bf16[32,4,8,64]{3,1,2,0:T(4,128)(2,1)S(1)} fusion(bf16[32,8,8,64]{3,2,0,1:T(8,128)(2,1)} %reshape.276, f32[32,8,4,8]{3,2,1,0:T(4,128)} %get-tuple-element.33, f32[32,8,4]{2,1,0:T(8,128)S(1)} %get-tuple-element.32), kind=kOutput, calls=%fused_computation.45 | convolution fusion | flops 1130496 | bytes 430080 | tf_op jit(solution)/shard_map/rhij,rjhd->rihd/dot_general | solution.py:63
  62.2 1.3 multiply_reduce_fusion.2
  64.4 1.6 %reshape.250 = bf16[128,512]{1,0:T(8,128)(2,1)} reshape(bf16[32,4,512]{2,1,0:T(4,128)(2,1)} %copy.107) | data formatting | bytes 262144 | tf_op jit(solution)/shard_map/reshape | solution.py:70
  66.0 1.8 %convolution_convert_fusion.10 = bf16[128,512]{1,0:T(8,128)(2,1)} fusion(bf16[128,512]{1,0:T(8,128)(2,1)} %reshape.250, bf16[1,512,512]{2,1,0:T(8,128)(2,1)S(1)} %copy-done.1), kind=kOutput, calls=%fused_computation.70 | convolution fusion | flops 67174400 | bytes 786432 | tf_op jit(solution)/shard_map/dot_general | solution.py:71
  67.8 1.8 %reshape.251 = bf16[32,4,8,64]{3,2,1,0:T(8,128)(2,1)} reshape(bf16[128,512]{1,0:T(8,128)(2,1)} %convolution_convert_fusion.10) | data formatting | bytes 262144 | tf_op jit(solution)/shard_map/reshape | solution.py:72
  69.5 1.2 fusion.118
  70.9 1.6 %fusion.26 = bf16[32,4,8,64]{3,0,2,1:T(8,128)(2,1)S(1)} fusion(f32[32,4,8]{0,2,1:T(8,128)S(1)} %fusion.88, f32[32,4,8,16]{0,3,2,1:T(8,128)S(1)} %get-tuple-element.37, f32[32,4,8]{0,2,1:T(8,128)S(1)} %broadcast_maximum_fusion.2, bf16[16,4,8,64]{3,2,1,0:T(8,128)(2,1)} %reshape.283), kind=kOutput, calls=%fused_computation.42 | convolution fusion | flops 12730368 | bytes 270336 | tf_op jit(solution)/shard_map/rghn,nghd->rghd/dot_general | solution.py:86
  73.2 1.8 %dot_general.130 = bf16[32,4,512]{2,0,1:T(8,128)(2,1)} reshape(bf16[32,4,8,64]{3,2,0,1:T(8,128)(2,1)} %copy.111) | data formatting | bytes 262144 | tf_op jit(solution)/shard_map/dot_general | solution.py:90
  75.1 1.2 fusion.37
  76.2 1.3 collective-permute-start.1
  77.5 0.9 fusion.93
  79.2 1.6 %constant_dynamic-slice_fusion.1 = bf16[1,32,4,512]{3,2,1,0:T(4,128)(2,1)} fusion(bf16[3,32,4,512]{3,2,1,0:T(4,128)(2,1)} %copy_dynamic-update-slice_fusion.2, s32[]{:T(128)S(6)} %min.15), kind=kLoop, calls=%fused_computation.189 | loop fusion | bytes 262148 | tf_op jit(solution)/shard_map/jit(dynamic_index_in_dim)/dynamic_slice | solution.py:95
  80.8 2.0 %collective-permute-done.1 = bf16[32,4,512]{2,0,1:T(8,128)(2,1)S(1)} collective-permute-done((bf16[32,4,512]{2,0,1:T(8,128)(2,1)S(1)}, bf16[32,4,512]{2,0,1:T(8,128)(2,1)S(1)}, u32[]{:S(2)}, u32[]{:S(2)}) %collective-permute-start.1) | collective-permute-done | bytes 131104 | tf_op jit(solution)/shard_map/ppermute | solution.py:15
  83.9 1.1 convolution_convert_fusion.1
  85.0 1.8 %reshape.253 = bf16[32,4,1536]{2,1,0:T(4,128)(2,1)} reshape(bf16[128,1536]{1,0:T(8,128)(2,1)} %convolution_convert_fusion.1) | data formatting | bytes 786432 | tf_op jit(solution)/shard_map/reshape | solution.py:52
  86.8 1.0 slice.111
  88.0 3.0 %all_gather.21 = bf16[32,8,1024]{2,0,1:T(8,128)(2,1)S(1)} all-gather(bf16[32,4,1024]{2,0,1:T(8,128)(2,1)S(1)} %copy.174), channel_id=1, replica_groups=mesh['groups'=2,'rows'=4,'section'=2,'feat'=2] {'feat'}, dimensions={1}, use_global_device_ids=true | all-gather | bytes 786432 | tf_op jit(solution)/shard_map/all_gather | solution.py:54
  91.9 2.1 %reshape.279 = bf16[32,8,8,64]{3,2,0,1:T(8,128)(2,1)} reshape(bf16[32,8,512]{2,0,1:T(8,128)(2,1)} %get-tuple-element.13) | data formatting | bytes 524288 | tf_op jit(solution)/shard_map/reshape | solution.py:56
  94.8 2.1 %reshape.278 = bf16[32,8,8,64]{3,2,0,1:T(8,128)(2,1)} reshape(bf16[32,8,512]{2,0,1:T(8,128)(2,1)} %get-tuple-element.14) | data formatting | bytes 524288 | tf_op jit(solution)/shard_map/reshape | solution.py:57
  96.9 2.7 %fusion.119 = (f32[32,8,4]{2,1,0:T(8,128)S(1)}, f32[32,8,4,8]{3,2,1,0:T(4,128)}) fusion(bf16[32,8,8,64]{3,2,0,1:T(8,128)(2,1)} %reshape.279, bf16[32,4,8,64]{3,2,1,0:T(8,128)(2,1)} %reshape.286, pred[4,8]{1,0:T(4,128)(4,1)S(1)} %copy-done.20), kind=kOutput, calls=%fused_computation.204 | convolution fusion | flops 1081351 | bytes 430112 | tf_op jit(solution)/shard_map/sub | solution.py:62
  99.6 1.8 %fusion.30 = bf16[32,4,8,64]{3,1,2,0:T(4,128)(2,1)S(1)} fusion(bf16[32,8,8,64]{3,2,0,1:T(8,128)(2,1)} %reshape.278, f32[32,8,4,8]{3,2,1,0:T(4,128)} %get-tuple-element.39, f32[32,8,4]{2,1,0:T(8,128)S(1)} %get-tuple-element.38), kind=kOutput, calls=%fused_computation.46 | convolution fusion | flops 1130496 | bytes 430080 | tf_op jit(solution)/shard_map/rhij,rjhd->rihd/dot_general | solution.py:63
  102.3 1.3 multiply_reduce_fusion.1
  104.5 1.6 %reshape.257 = bf16[128,512]{1,0:T(8,128)(2,1)} reshape(bf16[32,4,512]{2,1,0:T(4,128)(2,1)} %copy.124) | data formatting | bytes 262144 | tf_op jit(solution)/shard_map/reshape | solution.py:70
  106.0 1.8 %convolution_convert_fusion.9 = bf16[128,512]{1,0:T(8,128)(2,1)} fusion(bf16[128,512]{1,0:T(8,128)(2,1)} %reshape.257, bf16[1,512,512]{2,1,0:T(8,128)(2,1)S(1)} %copy-done.1), kind=kOutput, calls=%fused_computation.69 | convolution fusion | flops 67174400 | bytes 786432 | tf_op jit(solution)/shard_map/dot_general | solution.py:71
  107.8 1.8 %reshape.258 = bf16[32,4,8,64]{3,2,1,0:T(8,128)(2,1)} reshape(bf16[128,512]{1,0:T(8,128)(2,1)} %convolution_convert_fusion.9) | data formatting | bytes 262144 | tf_op jit(solution)/shard_map/reshape | solution.py:72
  109.6 1.2 fusion.120
  110.9 1.6 %fusion.25 = bf16[32,4,8,64]{3,0,2,1:T(8,128)(2,1)S(1)} fusion(f32[32,4,8]{0,2,1:T(8,128)S(1)} %fusion.89, f32[32,4,8,16]{0,3,2,1:T(8,128)S(1)} %get-tuple-element.43, f32[32,4,8]{0,2,1:T(8,128)S(1)} %broadcast_maximum_fusion.1, bf16[16,4,8,64]{3,2,1,0:T(8,128)(2,1)} %reshape.283), kind=kOutput, calls=%fused_computation.41 | convolution fusion | flops 12730368 | bytes 270336 | tf_op jit(solution)/shard_map/rghn,nghd->rghd/dot_general | solution.py:86
  113.3 1.8 %dot_general.140 = bf16[32,4,512]{2,0,1:T(8,128)(2,1)} reshape(bf16[32,4,8,64]{3,2,0,1:T(8,128)(2,1)} %copy.128) | data formatting | bytes 262144 | tf_op jit(solution)/shard_map/dot_general | solution.py:90
  115.1 1.2 fusion.38
  116.3 1.3 collective-permute-start.2
  117.6 0.9 fusion.92
  119.3 1.6 %constant_dynamic-slice_fusion = bf16[1,32,4,512]{3,2,1,0:T(4,128)(2,1)} fusion(bf16[3,32,4,512]{3,2,1,0:T(4,128)(2,1)} %copy_dynamic-update-slice_fusion.1, s32[]{:T(128)S(6)} %min.16), kind=kLoop, calls=%fused_computation.188 | loop fusion | bytes 262148 | tf_op jit(solution)/shard_map/jit(dynamic_index_in_dim)/dynamic_slice | solution.py:95
  120.9 2.0 %collective-permute-done.2 = bf16[32,4,512]{2,0,1:T(8,128)(2,1)S(1)} collective-permute-done((bf16[32,4,512]{2,0,1:T(8,128)(2,1)S(1)}, bf16[32,4,512]{2,0,1:T(8,128)(2,1)S(1)}, u32[]{:S(2)}, u32[]{:S(2)}) %collective-permute-start.2) | collective-permute-done | bytes 131104 | tf_op jit(solution)/shard_map/ppermute | solution.py:15
  123.9 1.1 convolution_convert_fusion
  125.1 1.8 %reshape.260 = bf16[32,4,1536]{2,1,0:T(4,128)(2,1)} reshape(bf16[128,1536]{1,0:T(8,128)(2,1)} %convolution_convert_fusion) | data formatting | bytes 786432 | tf_op jit(solution)/shard_map/reshape | solution.py:52
  126.9 1.0 slice.115
  128.0 3.3 %all_gather.22 = bf16[32,8,1024]{2,0,1:T(8,128)(2,1)S(1)} all-gather(bf16[32,4,1024]{2,0,1:T(8,128)(2,1)S(1)} %copy.176), channel_id=1, replica_groups=mesh['groups'=2,'rows'=4,'section'=2,'feat'=2] {'feat'}, dimensions={1}, use_global_device_ids=true | all-gather | bytes 786432 | tf_op jit(solution)/shard_map/all_gather | solution.py:54
  132.2 2.1 %reshape.281 = bf16[32,8,8,64]{3,2,0,1:T(8,128)(2,1)} reshape(bf16[32,8,512]{2,0,1:T(8,128)(2,1)} %get-tuple-element.11) | data formatting | bytes 524288 | tf_op jit(solution)/shard_map/reshape | solution.py:56
  135.1 2.1 %reshape.280 = bf16[32,8,8,64]{3,2,0,1:T(8,128)(2,1)} reshape(bf16[32,8,512]{2,0,1:T(8,128)(2,1)} %get-tuple-element.12) | data formatting | bytes 524288 | tf_op jit(solution)/shard_map/reshape | solution.py:57
  137.2 2.7 %fusion.121 = (f32[32,8,4]{2,1,0:T(8,128)S(1)}, f32[32,8,4,8]{3,2,1,0:T(4,128)}) fusion(bf16[32,8,8,64]{3,2,0,1:T(8,128)(2,1)} %reshape.281, bf16[32,4,8,64]{3,2,1,0:T(8,128)(2,1)} %reshape.287, pred[4,8]{1,0:T(4,128)(4,1)S(1)} %copy-done.20), kind=kOutput, calls=%fused_computation.206 | convolution fusion | flops 1081351 | bytes 430112 | tf_op jit(solution)/shard_map/sub | solution.py:62
  139.9 1.8 %fusion.31 = bf16[32,4,8,64]{3,1,2,0:T(4,128)(2,1)S(1)} fusion(bf16[32,8,8,64]{3,2,0,1:T(8,128)(2,1)} %reshape.280, f32[32,8,4,8]{3,2,1,0:T(4,128)} %get-tuple-element.45, f32[32,8,4]{2,1,0:T(8,128)S(1)} %get-tuple-element.44), kind=kOutput, calls=%fused_computation.47 | convolution fusion | flops 1130496 | bytes 430080 | tf_op jit(solution)/shard_map/rhij,rjhd->rihd/dot_general | solution.py:63
  142.6 1.3 multiply_reduce_fusion
  (138 shorter events, 25.6 us)
Async XLA Ops:
  0.0 3.1 %copy-start = (bf16[1,512,1536]{2,1,0:T(8,128)(2,1)S(1)}, bf16[1,512,1536]{2,1,0:T(8,128)(2,1)}, u32[]{:S(2)}) copy-start(bf16[1,512,1536]{2,1,0:T(8,128)(2,1)} %param.11) | copy-start | bytes 4718596
  2.9 0.8 copy-start.15
  2.9 9.1 %copy-start.13 = (f32[1,1,512]{2,1,0:T(1,128)}, f32[1,1,512]{2,1,0:T(1,128)S(1)}, u32[]{:S(2)}) copy-start(f32[1,1,512]{2,1,0:T(1,128)S(1)} %get-tuple-element.24) | copy-start | bytes 6148
  6.4 1.6 %copy-start.18 = (s32[8,8]{1,0:T(8,128)S(1)}, s32[8,8]{1,0:T(8,128)}, u32[]{:S(2)}) copy-start(s32[8,8]{1,0:T(8,128)} %param.10) | copy-start | bytes 772
  8.0 1.6 %copy-start.11 = (bf16[32,8,8,64]{3,2,0,1:T(8,128)(2,1)S(1)}, bf16[32,8,8,64]{3,2,0,1:T(8,128)(2,1)}, u32[]{:S(2)}) copy-start(bf16[32,8,8,64]{3,2,0,1:T(8,128)(2,1)} %reshape.274) | copy-start | bytes 786436
  8.1 1.6 %copy-start.19 = (pred[4,8]{1,0:T(4,128)(4,1)}, pred[4,8]{1,0:T(4,128)(4,1)S(1)}, u32[]{:S(2)}) copy-start(pred[4,8]{1,0:T(4,128)(4,1)S(1)} %fusion.106) | copy-start | bytes 100
  9.6 2.0 %copy-start.2 = (bf16[1,512,512]{2,1,0:T(8,128)(2,1)S(1)}, bf16[1,512,512]{2,1,0:T(8,128)(2,1)}, u32[]{:S(2)}) copy-start(bf16[1,512,512]{2,1,0:T(8,128)(2,1)} %param.12) | copy-start | bytes 1572868
  11.3 1.0 copy-start.1
  11.6 1.2 copy-start.17
  24.8 1.7 %copy-start.9 = (f32[32,4,8,16]{0,3,2,1:T(8,128)}, f32[32,4,8,16]{0,3,2,1:T(8,128)S(1)}, u32[]{:S(2)}) copy-start(f32[32,4,8,16]{0,3,2,1:T(8,128)S(1)} %get-tuple-element.31) | copy-start | bytes 196612
  26.6 4.3 %copy-start.3 = (bf16[1,512,512]{2,1,0:T(8,128)(2,1)S(1)}, bf16[1,512,512]{2,1,0:T(8,128)(2,1)}, u32[]{:S(2)}) copy-start(bf16[1,512,512]{2,1,0:T(8,128)(2,1)} %param.14) | copy-start | bytes 1572868
  29.1 11.2 %copy-start.16 = (f32[1,1,512]{2,1,0:T(1,128)S(1)}, f32[1,1,512]{2,1,0:T(1,128)}, u32[]{:S(2)}) copy-start(f32[1,1,512]{2,1,0:T(1,128)} %copy-done.15) | copy-start | bytes 6148
  32.8 5.9 %collective-permute-start = (bf16[32,4,512]{2,0,1:T(8,128)(2,1)}, bf16[32,4,512]{2,0,1:T(8,128)(2,1)S(1)}, u32[]{:S(2)}, u32[]{:S(2)}) collective-permute-start(bf16[32,4,512]{2,0,1:T(8,128)(2,1)} %fusion.36), channel_id=1, source_target_pairs={{0,2},{1,3},{4,6},{5,7},{8,10},{9,11},{12,14},{13,15},{16,18},{17,... | collective-permute-start | bytes 393224 | tf_op jit(solution)/shard_map/ppermute | solution.py:15
  39.7 0.7 copy-start.7
  44.6 9.2 %slice-start = ((bf16[32,4,1536]{2,1,0:T(4,128)(2,1)}), bf16[32,4,512]{2,1,0:T(4,128)(2,1)S(1)}, s32[]{:S(2)}) async-start(bf16[32,4,1536]{2,1,0:T(4,128)(2,1)} %reshape.246), calls=%async_computation | async-start | bytes 262144 | tf_op jit(solution)/shard_map/slice | solution.py:53
  50.9 5.9 %copy-start.20 = (pred[4,8]{1,0:T(4,128)(4,1)S(1)}, pred[4,8]{1,0:T(4,128)(4,1)}, u32[]{:S(2)}) copy-start(pred[4,8]{1,0:T(4,128)(4,1)} %copy-done.19) | copy-start | bytes 100
  61.3 2.2 %copy-start.14 = (f32[1,1,512]{2,1,0:T(1,128)S(1)}, f32[1,1,512]{2,1,0:T(1,128)}, u32[]{:S(2)}) copy-start(f32[1,1,512]{2,1,0:T(1,128)} %copy-done.13) | copy-start | bytes 6148
  75.1 7.8 %copy-start.4 = (bf16[1,32,4,512]{3,2,1,0:T(4,128)(2,1)S(1)}, bf16[1,32,4,512]{3,2,1,0:T(4,128)(2,1)}, u32[]{:S(2)}) copy-start(bf16[1,32,4,512]{3,2,1,0:T(4,128)(2,1)} %get-tuple-element.19) | copy-start | bytes 393220
  76.2 6.6 %collective-permute-start.1 = (bf16[32,4,512]{2,0,1:T(8,128)(2,1)S(1)}, bf16[32,4,512]{2,0,1:T(8,128)(2,1)S(1)}, u32[]{:S(2)}, u32[]{:S(2)}) collective-permute-start(bf16[32,4,512]{2,0,1:T(8,128)(2,1)S(1)} %fusion.37), channel_id=1, source_target_pairs={{0,2},{1,3},{4,6},{5,7},{8,10},{9,11},{12,14},{13,15},{16,18},{17,... | collective-permute-start | bytes 393224 | tf_op jit(solution)/shard_map/ppermute | solution.py:15
  83.0 0.7 copy-start.8
  87.9 6.1 %slice-start.1 = ((bf16[32,4,1536]{2,1,0:T(4,128)(2,1)}), bf16[32,4,512]{2,1,0:T(4,128)(2,1)S(1)}, s32[]{:S(2)}) async-start(bf16[32,4,1536]{2,1,0:T(4,128)(2,1)} %reshape.253), calls=%async_computation.1 | async-start | bytes 262144 | tf_op jit(solution)/shard_map/slice | solution.py:53
  115.1 7.8 %copy-start.5 = (bf16[1,32,4,512]{3,2,1,0:T(4,128)(2,1)S(1)}, bf16[1,32,4,512]{3,2,1,0:T(4,128)(2,1)}, u32[]{:S(2)}) copy-start(bf16[1,32,4,512]{3,2,1,0:T(4,128)(2,1)} %get-tuple-element.19) | copy-start | bytes 393220
  116.3 6.6 %collective-permute-start.2 = (bf16[32,4,512]{2,0,1:T(8,128)(2,1)S(1)}, bf16[32,4,512]{2,0,1:T(8,128)(2,1)S(1)}, u32[]{:S(2)}, u32[]{:S(2)}) collective-permute-start(bf16[32,4,512]{2,0,1:T(8,128)(2,1)S(1)} %fusion.38), channel_id=1, source_target_pairs={{0,2},{1,3},{4,6},{5,7},{8,10},{9,11},{12,14},{13,15},{16,18},{17,... | collective-permute-start | bytes 393224 | tf_op jit(solution)/shard_map/ppermute | solution.py:15
  123.0 0.7 copy-start.6
  128.0 6.3 %slice-start.2 = ((bf16[32,4,1536]{2,1,0:T(4,128)(2,1)}), bf16[32,4,512]{2,1,0:T(4,128)(2,1)S(1)}, s32[]{:S(2)}) async-start(bf16[32,4,1536]{2,1,0:T(4,128)(2,1)} %reshape.260), calls=%async_computation.2 | async-start | bytes 262144 | tf_op jit(solution)/shard_map/slice | solution.py:53
  143.9 1.1 copy-start.12
  145.0 1.0 copy-start.10
where the time goes:
time: 149 us; the launch traced here: 147 us
  local copies, waits for them, and re-layouts  65.1 us (44%)
  matrix products  41.6 us (28%)
  blocking collectives  25.9 us (17%)
  waiting for transfers between devices  5.32 us (4%)
  other arithmetic  4.52 us (3%)
  starting transfers between devices  3.86 us (3%)
    all_gather x4, blocking collectives, per_device(): pairs = lax.all_gather(qkv[:, :, width:], 'feat', axis=1, tiled=True)  15 us
    all_gather x1, blocking collectives, per_device(): piece = lax.all_gather(cache, 'rows', axis=1, tiled=True)  10.9 us
    sub x4, matrix products, per_device(): weights = jax.nn.softmax(scores, axis=-1).astype(jnp.bfloat16)  9.65 us
    reshape x4, local copies, waits for them, and re-layouts, per_device(): values = pairs[:, :, width:].reshape(test_n, groups, heads, head_dim)  7.3 us
    dot_general x4, matrix products, per_device(): jnp.einsum('rhij,rjhd->rihd', weights, values, preferred_element_type=jnp...  7.14 us
    reshape x4, local copies, waits for them, and re-layouts, per_device(): keys = pairs[:, :, :width].reshape(test_n, groups, heads, head_dim)  6.44 us
    dot_general x4, local copies, waits for them, and re-layouts, per_device(): term = jnp.dot(item_mix, witem, preferred_element_type=jnp.float32)  5.67 us
    reshape x4, local copies, waits for them, and re-layouts, per_device(): qkv = qkv.reshape(test_n, group_dev, 3 * width)  5.63 us
  transfers between devices with their start and end apart: 3, of which 3 were waited for; matrix products, arithmetic and copies ran while one was open for 7% of the time, Pallas kernels for 0%

commit v1 on v0

v1 whole, which is shorter than its diff:
```python
import functools

import jax
import jax.numpy as jnp
from jax import lax
from jax.experimental import pallas as pl
from jax.experimental.pallas import tpu as pltpu
from jax.sharding import PartitionSpec as P

HEADS = 8
NEG = -1e30
VMEM = pltpu.MemorySpace.VMEM


def whole():
    return pl.BlockSpec(memory_space=VMEM)


def prep_kernel(half, x_ref, own_ref, send_ref, wide):
    micro, _, group_dev, _ = x_ref.shape
    feat = lax.axis_index("feat")
    for m in range(micro):
        for part, out in ((feat, own_ref), (1 - feat, send_ref)):
            for r in range(half):
                row = x_ref[m, part * half + r].astype(jnp.float32)
                wide[r * group_dev:(r + 1) * group_dev, :] = row
            out[m] = wide[...].astype(jnp.bfloat16)


def prep_cache_kernel(c_ref, out_ref, wide):
    _, _, rows, group_dev, _ = c_ref.shape
    for kv in range(2):
        for n in range(rows):
            wide[n * group_dev:(n + 1) * group_dev, :] = c_ref[0, kv, n].astype(jnp.float32)
        out_ref[kv] = wide[...].astype(jnp.bfloat16)


def group_of(index, dim, own_count, group_dev, feat, shape):
    at = lax.broadcasted_iota(jnp.int32, shape, dim)
    side = jnp.where(at < own_count, feat, 1 - feat)
    return side * group_dev + lax.rem(at, group_dev)


def norm(x, gain):
    mean_sq = jnp.mean(x * x, axis=-1, keepdims=True)
    return x * lax.rsqrt(mean_sq + 1e-06) * gain


def attend(query, keys, values, masked, low):
    tokens, width = query.shape
    lanes = 128
    key_n = keys.shape[0]
    ones = jnp.ones((key_n, lanes), jnp.bfloat16)
    zero = jnp.zeros((), jnp.bfloat16)
    outs = []
    for pair in range(width // lanes):
        span = slice(pair * lanes, (pair + 1) * lanes)
        q = query[:, span]
        stacked = jnp.concatenate([jnp.where(low, q, zero), jnp.where(low, zero, q)], axis=0)
        scores = lax.dot_general(stacked, keys[:, span], (((1,), (1,)), ((), ())), preferred_element_type=jnp.float32)
        scores = jnp.where(masked, NEG, scores)
        expo = jnp.exp(scores - jnp.max(scores, axis=-1, keepdims=True)).astype(jnp.bfloat16)
        extended = jnp.concatenate([values[:, span], ones], axis=1)
        mixed = jnp.dot(expo, extended, preferred_element_type=jnp.float32)
        mixed = mixed[:, :lanes] / mixed[:, lanes:]
        outs.append(jnp.where(low, mixed[:tokens], mixed[tokens:]).astype(jnp.bfloat16))
    return jnp.concatenate(outs, axis=1)


def layer(h, keys, values, feat_mask, item_mask, wqkv, wout, wquery, witem, gains):
    tokens, width = h.shape
    head_dim = width // HEADS
    scale = 1.0 / head_dim**0.5
    low = lax.rem(lax.broadcasted_iota(jnp.int32, (tokens, 128), 1), 128) < head_dim
    a = norm(h, gains[0:1, :]).astype(jnp.bfloat16)
    qkv = jnp.dot(a, wqkv[...], preferred_element_type=jnp.float32)
    query = (qkv[:, :width].astype(jnp.bfloat16) * scale).astype(jnp.bfloat16)
    rest = qkv[:, width:].astype(jnp.bfloat16)
    mixed = attend(query, rest[:, :width], rest[:, width:], feat_mask, low)
    h1 = h + jnp.dot(mixed, wout[...], preferred_element_type=jnp.float32)
    b = norm(h1, gains[1:2, :]).astype(jnp.bfloat16)
    item_q = jnp.dot(b, wquery[...], preferred_element_type=jnp.float32)
    item_q = (item_q.astype(jnp.bfloat16) * scale).astype(jnp.bfloat16)
    item_mix = attend(item_q, keys, values, item_mask, low)
    return h1 + jnp.dot(item_mix, witem[...], preferred_element_type=jnp.float32)


def layer_kernel(phase, pieces, group_dev, *refs):
    first, second, previous = refs[:3]
    near, far = refs[3:3 + pieces], refs[3 + pieces:3 + 2 * pieces]
    pattern, wqkv, wout, wquery, witem, gains, out_ref = refs[3 + 2 * pieces:]
    section = lax.axis_index("section")
    feat = lax.axis_index("feat")
    tokens = out_ref.shape[0]
    half = tokens // 2
    groups = 2 * group_dev

    @pl.when(section == phase)
    def _():
        if phase == 0:
            h = jnp.concatenate([first[...], second[...]], axis=0).astype(jnp.float32)
        else:
            h = first[...].astype(jnp.float32)
        keys = jnp.concatenate([r[0] for r in near] + [r[0] for r in far], axis=0)
        values = jnp.concatenate([r[1] for r in near] + [r[1] for r in far], axis=0)
        key_n = keys.shape[0]
        eye = group_of(None, 0, half, group_dev, feat, (tokens, groups)) == lax.broadcasted_iota(jnp.int32, (tokens, groups), 1)
        one_hot = eye.astype(jnp.float32)
        table = (pattern[...] != 0).astype(jnp.float32)
        spread = jnp.dot(one_hot, table, preferred_element_type=jnp.float32)
        full = lax.dot_general(spread, one_hot, (((1,), (1,)), ((), ())), preferred_element_type=jnp.float32)
        at_i = lax.broadcasted_iota(jnp.int32, (tokens, tokens), 0)
        at_j = lax.broadcasted_iota(jnp.int32, (tokens, tokens), 1)
        same_row = lax.rem(at_i, half) // group_dev == lax.rem(at_j, half) // group_dev
        allowed = (same_row & (full > 0.5)) | (at_i == at_j)
        feat_mask = jnp.concatenate([~allowed, ~allowed], axis=0)
        item_shape = (tokens, key_n)
        other = group_of(None, 0, half, group_dev, feat, item_shape) != group_of(
            None, 1, key_n // 2, group_dev, feat, item_shape
        )
        item_mask = jnp.concatenate([other, other], axis=0)
        out = layer(h, keys, values, feat_mask, item_mask, wqkv.at[0], wout.at[0], wquery.at[0], witem.at[0], gains.at[0])
        out_ref[...] = out.astype(jnp.bfloat16)

    if phase > 0:

        @pl.when(section != phase)
        def _():
            out_ref[...] = previous[...]


def final_kernel(half, recv_ref, *refs):
    own_refs, out_ref, wide = refs[:-2], refs[-2], refs[-1]
    micro, _, group_dev, _ = out_ref.shape
    feat = lax.axis_index("feat")
    tokens = half * group_dev
    for m in range(micro):
        for part, value in ((feat, own_refs[m][:tokens]), (1 - feat, recv_ref[m])):
            wide[...] = value.astype(jnp.float32)
            for r in range(half):
                out_ref[m, part * half + r] = wide[r * group_dev:(r + 1) * group_dev, :].astype(jnp.bfloat16)


def per_device(test_rows, train_cache, pattern, feat_qkv, feat_out, item_query, item_out, gains):
    micro, test_n, group_dev, width = test_rows.shape
    sections = lax.axis_size("section")
    rows = lax.axis_size("rows")
    half = test_n // 2
    tokens = half * group_dev
    bf16 = jnp.bfloat16
    swap = [(0, 1), (1, 0)]
    own, send = pl.pallas_call(
        functools.partial(prep_kernel, half),
        out_shape=[jax.ShapeDtypeStruct((micro, tokens, width), bf16)] * 2,
        in_specs=[whole()],
        out_specs=[whole()] * 2,
        scratch_shapes=[pltpu.VMEM((tokens, width), jnp.float32)],
        name="prep_rows",
    )(test_rows)
    other = lax.ppermute(send, "feat", swap)
    count = train_cache.shape[2] * group_dev
    cache = pl.pallas_call(
        prep_cache_kernel,
        out_shape=jax.ShapeDtypeStruct((2, count, width), bf16),
        in_specs=[whole()],
        out_specs=whole(),
        scratch_shapes=[pltpu.VMEM((count, width), jnp.float32)],
        name="prep_cache",
    )(train_cache)
    near = [cache]
    for shift in range(1, rows):
        near.append(lax.ppermute(cache, "rows", [(i, (i + shift) % rows) for i in range(rows)]))
    far = [lax.ppermute(piece, "feat", swap) for piece in near]
    weights = (pattern, feat_qkv, feat_out, item_query, item_out, gains)
    results = [None] * micro
    arriving = [None] * micro
    for phase in range(sections):
        for m in range(micro):
            if phase == 0:
                first, second, previous = own[m], other[m], own[m]
            else:
                first, second, previous = arriving[m], arriving[m], results[m]
            operands = (first, second, previous, *near, *far, *weights)
            results[m] = pl.pallas_call(
                functools.partial(layer_kernel, phase, len(near), group_dev),
                out_shape=jax.ShapeDtypeStruct((2 * tokens, width), bf16),
                in_specs=[whole()] * len(operands),
                out_specs=whole(),
                name=f"layer_{phase}_{m}",
                compiler_params=pltpu.CompilerParams(vmem_limit_bytes=32 * 1024 * 1024),
            )(*operands)
            if phase + 1 < sections:
                arriving[m] = lax.ppermute(results[m], "section", [(phase, phase + 1)])
    leaving = jnp.stack([r[tokens:] for r in results])
    entering = lax.ppermute(leaving, "feat", swap)
    out = pl.pallas_call(
        functools.partial(final_kernel, half),
        out_shape=jax.ShapeDtypeStruct((micro, test_n, group_dev, width), bf16),
        in_specs=[whole()] * (1 + micro),
        out_specs=whole(),
        scratch_shapes=[pltpu.VMEM((tokens, width), jnp.float32)],
        name="assemble",
    )(entering, *results)
    return out[None]


def solution(mesh):
    return jax.shard_map(
        per_device,
        mesh=mesh,
        in_specs=(
            P(None, ("groups", "rows"), "feat", None),
            P("section", None, ("groups", "rows"), "feat", None),
            P(),
            P("section", None, None),
            P("section", None, None),
            P("section", None, None),
            P("section", None, None),
            P("section", None, None),
        ),
        out_specs=P("section", None, ("groups", "rows"), "feat", None),
        check_vma=False,
    )
```

time: 149 us -> 39.5 us (0.27)
  local copies, waits for them, and re-layouts: 65.1 us -> 6.23 us
  matrix products: 41.6 us -> 0 us
  blocking collectives: 25.9 us -> 0 us
  Pallas kernels: 0 us -> 12.4 us
  starting transfers between devices: 3.86 us -> 12.4 us
  other arithmetic: 4.52 us -> 0.03 us
  waiting for transfers between devices: 5.32 us -> 7.77 us
    dot_general x28 -> x0, matrix products: 31.9 us -> none  [the longest x4 7.14 us: per_device(): jnp.einsum('rhij,rjhd->rihd', weights, values, preferred_element_type=jnp...]
    reshape x28 -> x0, local copies, waits for them, and re-layouts: 31.2 us -> none  [the longest x4 7.3 us: per_device(): values = pairs[:, :, width:].reshape(test_n, groups, heads, head_dim)]
    all_gather x5 -> x0, blocking collectives: 25.9 us -> none  [the longest x4 15 us: per_device(): pairs = lax.all_gather(qkv[:, :, width:], 'feat', axis=1, tiled=True)]
    pallas_call x0 -> x9, Pallas kernels: none -> 12.4 us  [the longest x6 7.03 us: per_device(): pl.pallas_call(functools.partial(layer_kernel, phase, len(near), group_de...]
    sub x4 -> x0, matrix products: 9.65 us -> none  [per_device(): weights = jax.nn.softmax(scores, axis=-1).astype(jnp.bfloat16)]
    slice x18 -> x0, local copies, waits for them, and re-layouts: 9.32 us -> none  [the longest x4 3.22 us: per_device(): pairs = lax.all_gather(qkv[:, :, width:], 'feat', axis=1, tiled=True)]
    ppermute x3 -> x12, starting transfers between devices: 3.86 us -> 12.4 us  [the longest x3 4 us: per_device(): arriving[m] = lax.ppermute(results[m], 'section', [(phase, phase + 1)])]
    dot_general x8 -> x0, local copies, waits for them, and re-layouts: 8.43 us -> none  [the longest x4 5.67 us: per_device(): term = jnp.dot(item_mix, witem, preferred_element_type=jnp.float32)]
  transfers between devices with their start and end apart: 3 -> 12, of which waited for: 3 -> 6; matrix products, arithmetic and copies ran while one was open for 7% -> 2% of each run, Pallas kernels for 0% -> 17%
where the time goes in v1:
time: 39.5 us; the launch traced here: 39 us
  Pallas kernels  12.4 us (31%)
  starting transfers between devices  12.4 us (31%)
  waiting for transfers between devices  7.77 us (20%)
  local copies, waits for them, and re-layouts  6.23 us (16%)
    pallas_call x6, Pallas kernels, per_device(): pl.pallas_call(functools.partial(layer_kernel, phase, len(near), group_de...  7.03 us
    ppermute x3, waiting for transfers between devices, per_device(): arriving[m] = lax.ppermute(results[m], 'section', [(phase, phase + 1)])  5.86 us
    unnamed x24, local copies, waits for them, and re-layouts  5.28 us
    ppermute x3, starting transfers between devices, per_device(): arriving[m] = lax.ppermute(results[m], 'section', [(phase, phase + 1)])  4 us
    ppermute x3, starting transfers between devices, per_device(): lax.ppermute(cache, 'rows', [(i, (i + shift) % rows) for i in range(rows)])  3.77 us
    ppermute x4, starting transfers between devices, per_device(): far = [lax.ppermute(piece, 'feat', swap) for piece in near]  2.74 us
    pallas_call x1, Pallas kernels, per_device(): pl.pallas_call(functools.partial(final_kernel, half), out_shape=jax.Shape...  1.99 us
    pallas_call x1, Pallas kernels, per_device(): pl.pallas_call(functools.partial(prep_kernel, half), out_shape=[jax.Shape...  1.9 us
  transfers between devices with their start and end apart: 12, of which 6 were waited for; matrix products, arithmetic and copies ran while one was open for 2% of the time, Pallas kernels for 17%

profile of v1, /device:TPU:7, one launch (start us, length us, event | category | flops | bytes accessed | tf_op | source)
XLA Modules:
  0.0 39.0 jit_solution(17265561413891386711)
XLA Ops:
  0.0 0.0 copy-start.3
  0.0 0.0 copy-start.2
  0.0 1.5 %prep_cache.1.refs_3_ = bf16[2,16,512]{2,1,0:T(8,128)(2,1)} custom-call(bf16[1,2,4,4,512]{4,3,2,1,0:T(4,128)(2,1)} %c_ref.1), custom_call_target="tpu_custom_call" | custom-call | tf_op jit(solution)/shard_map/prep_cache/pallas_call | solution.py:162
  1.5 0.7 %collective-permute-start.4 = (bf16[2,16,512]{2,1,0:T(8,128)(2,1)}, bf16[2,16,512]{2,1,0:T(8,128)(2,1)S(1)}, u32[]{:S(2)}, u32[]{:S(2)}) collective-permute-start(bf16[2,16,512]{2,1,0:T(8,128)(2,1)} %prep_cache.1.refs_3_), channel_id=1, source_target_pairs={{0,1},{1,0},{2,3},{3,2},{4,5},{5,4},{6,7},{7,6},{8,9},{9,8},{10,11... | collective-permute-start | bytes 98312 | tf_op jit(solution)/shard_map/ppermute | solution.py:173
  2.2 3.3 %collective-permute-start.3 = (bf16[2,16,512]{2,1,0:T(8,128)(2,1)}, bf16[2,16,512]{2,1,0:T(8,128)(2,1)S(1)}, u32[]{:S(2)}, u32[]{:S(2)}) collective-permute-start(bf16[2,16,512]{2,1,0:T(8,128)(2,1)} %prep_cache.1.refs_3_), channel_id=1, source_target_pairs={{0,12},{4,0},{8,4},{12,8},{1,13},{5,1},{9,5},{13,9},{2,14},{6,2},{... | collective-permute-start | bytes 98312 | tf_op jit(solution)/shard_map/ppermute | solution.py:172
  5.5 0.0 collective-permute-start.2
  5.5 0.5 %collective-permute-start.1 = (bf16[2,16,512]{2,1,0:T(8,128)(2,1)}, bf16[2,16,512]{2,1,0:T(8,128)(2,1)S(1)}, u32[]{:S(2)}, u32[]{:S(2)}) collective-permute-start(bf16[2,16,512]{2,1,0:T(8,128)(2,1)} %prep_cache.1.refs_3_), channel_id=1, source_target_pairs={{0,4},{4,8},{8,12},{12,0},{1,5},{5,9},{9,13},{13,1},{2,6},{6,10},{... | collective-permute-start | bytes 98312 | tf_op jit(solution)/shard_map/ppermute | solution.py:172
  5.9 1.9 %prep_rows.1 = (bf16[3,64,512]{2,1,0:T(8,128)(2,1)}, bf16[3,64,512]{2,1,0:T(8,128)(2,1)}) custom-call(bf16[3,32,4,512]{3,2,1,0:T(4,128)(2,1)} %x_ref.1), custom_call_target="tpu_custom_call" | custom-call | tf_op jit(solution)/shard_map/prep_rows/pallas_call | solution.py:152
  7.8 0.8 %collective-permute-start = (bf16[3,64,512]{2,1,0:T(8,128)(2,1)}, bf16[3,64,512]{2,1,0:T(8,128)(2,1)S(1)}, u32[]{:S(2)}, u32[]{:S(2)}) collective-permute-start(bf16[3,64,512]{2,1,0:T(8,128)(2,1)} %get-tuple-element.8), channel_id=1, source_target_pairs={{0,1},{1,0},{2,3},{3,2},{4,5},{5,4},{6,7},{7,6},{8,9},{9,8},{10,11... | collective-permute-start | bytes 589832 | tf_op jit(solution)/shard_map/ppermute | solution.py:160
  8.7 0.9 %slice_bitcast_fusion.8 = (bf16[64,512]{1,0:T(8,128)(2,1)S(1)}, bf16[64,512]{1,0:T(8,128)(2,1)S(1)}, bf16[64,512]{1,0:T(8,128)(2,1)S(1)}) fusion(bf16[3,64,512]{2,1,0:T(8,128)(2,1)} %get-tuple-element.7), kind=kLoop, calls=%fused_computation.9 | loop fusion | bytes 393216 | tf_op jit(solution)/shard_map/squeeze | solution.py:180
  9.6 0.0 collective-permute-done.3.refs_6_
  9.6 0.1 collective-permute-start.7
  9.7 0.0 collective-permute-done.2.refs_5_
  9.7 1.4 %collective-permute-start.6 = (bf16[2,16,512]{2,1,0:T(8,128)(2,1)S(1)}, bf16[2,16,512]{2,1,0:T(8,128)(2,1)S(1)}, u32[]{:S(2)}, u32[]{:S(2)}) collective-permute-start(bf16[2,16,512]{2,1,0:T(8,128)(2,1)S(1)} %collective-permute-done.2.refs_5_), channel_id=1, source_target_pairs={{0,1},{1,0},{2,3},{3,2},{4,5},{5,4},{6,7},{7,6},{8,9},{9,8},{10,11... | collective-permute-start | bytes 98312 | tf_op jit(solution)/shard_map/ppermute | solution.py:173
  11.1 0.0 collective-permute-done.1.refs_4_
  11.1 0.5 %collective-permute-start.5 = (bf16[2,16,512]{2,1,0:T(8,128)(2,1)S(1)}, bf16[2,16,512]{2,1,0:T(8,128)(2,1)S(1)}, u32[]{:S(2)}, u32[]{:S(2)}) collective-permute-start(bf16[2,16,512]{2,1,0:T(8,128)(2,1)S(1)} %collective-permute-done.1.refs_4_), channel_id=1, source_target_pairs={{0,1},{1,0},{2,3},{3,2},{4,5},{5,4},{6,7},{7,6},{8,9},{9,8},{10,11... | collective-permute-start | bytes 98312 | tf_op jit(solution)/shard_map/ppermute | solution.py:173
  11.7 0.0 collective-permute-done
  11.7 0.0 collective-permute-done.4.refs_7_
  11.7 0.0 collective-permute-done.7.refs_10_
  11.7 0.3 collective-permute-done.6.refs_9_
  12.0 0.6 %collective-permute-done.5.refs_8_ = bf16[2,16,512]{2,1,0:T(8,128)(2,1)S(1)} collective-permute-done((bf16[2,16,512]{2,1,0:T(8,128)(2,1)S(1)}, bf16[2,16,512]{2,1,0:T(8,128)(2,1)S(1)}, u32[]{:S(2)}, u32[]{:S(2)}) %collective-permute-start.5) | collective-permute-done | bytes 32800 | tf_op jit(solution)/shard_map/ppermute | solution.py:173
  12.6 0.0 copy-done.3
  12.6 0.0 copy-done.2
  12.6 0.0 copy-start
  12.6 1.4 %copy-done = bf16[1,512,1536]{2,1,0:T(8,128)(2,1)S(1)} copy-done((bf16[1,512,1536]{2,1,0:T(8,128)(2,1)S(1)}, bf16[1,512,1536]{2,1,0:T(8,128)(2,1)}, u32[]{:S(2)}) %copy-start) | copy-done | bytes 1572888
  14.0 0.0 copy-start.4
  14.0 1.0 %copy-done.4 = bf16[1,512,512]{2,1,0:T(8,128)(2,1)S(1)} copy-done((bf16[1,512,512]{2,1,0:T(8,128)(2,1)S(1)}, bf16[1,512,512]{2,1,0:T(8,128)(2,1)}, u32[]{:S(2)}) %copy-start.4) | copy-done | bytes 524312
  15.0 0.0 copy-start.5
  15.0 0.8 %copy-done.5 = bf16[2,16,512]{2,1,0:T(8,128)(2,1)S(1)} copy-done((bf16[2,16,512]{2,1,0:T(8,128)(2,1)S(1)}, bf16[2,16,512]{2,1,0:T(8,128)(2,1)}, u32[]{:S(2)}) %copy-start.5) | copy-done | bytes 32792
  15.8 0.0 copy-start.9
  15.8 0.7 %copy-done.9 = s32[8,8]{1,0:T(8,128)S(1)} copy-done((s32[8,8]{1,0:T(8,128)S(1)}, s32[8,8]{1,0:T(8,128)}, u32[]{:S(2)}) %copy-start.9) | copy-done | bytes 280
  16.5 0.0 copy-start.10
  16.5 0.7 %copy-done.10 = f32[1,2,512]{2,1,0:T(2,128)S(1)} copy-done((f32[1,2,512]{2,1,0:T(2,128)S(1)}, f32[1,2,512]{2,1,0:T(2,128)}, u32[]{:S(2)}) %copy-start.10) | copy-done | bytes 4120
  17.1 0.0 copy-start.1
  17.1 1.4 %collective-permute-start.9 = (bf16[128,512]{1,0:T(8,128)(2,1)S(1)}, bf16[128,512]{1,0:T(8,128)(2,1)S(1)}, u32[]{:S(2)}, u32[]{:S(2)}) collective-permute-start(bf16[128,512]{1,0:T(8,128)(2,1)S(1)} %layer_0_1.1.refs_2_), channel_id=1, source_target_pairs={{0,2},{1,3},{4,6},{5,7},{8,10},{9,11},{12,14},{13,15},{16,18},{17,... | collective-permute-start | bytes 393224 | tf_op jit(solution)/shard_map/ppermute | solution.py:193
  18.6 0.0 copy-done.1
  18.6 1.3 %collective-permute-start.10 = (bf16[128,512]{1,0:T(8,128)(2,1)S(1)}, bf16[128,512]{1,0:T(8,128)(2,1)S(1)}, u32[]{:S(2)}, u32[]{:S(2)}) collective-permute-start(bf16[128,512]{1,0:T(8,128)(2,1)S(1)} %layer_0_2.1.refs_2_), channel_id=1, source_target_pairs={{0,2},{1,3},{4,6},{5,7},{8,10},{9,11},{12,14},{13,15},{16,18},{17,... | collective-permute-start | bytes 393224 | tf_op jit(solution)/shard_map/ppermute | solution.py:193
  19.9 1.3 %collective-permute-start.8 = (bf16[128,512]{1,0:T(8,128)(2,1)S(1)}, bf16[128,512]{1,0:T(8,128)(2,1)S(1)}, u32[]{:S(2)}, u32[]{:S(2)}) collective-permute-start(bf16[128,512]{1,0:T(8,128)(2,1)S(1)} %layer_0_0.1.refs_2_), channel_id=1, source_target_pairs={{0,2},{1,3},{4,6},{5,7},{8,10},{9,11},{12,14},{13,15},{16,18},{17,... | collective-permute-start | bytes 393224 | tf_op jit(solution)/shard_map/ppermute | solution.py:193
  21.2 3.3 %collective-permute-done.9.refs_0_.refs_1_ = bf16[128,512]{1,0:T(8,128)(2,1)S(1)} collective-permute-done((bf16[128,512]{1,0:T(8,128)(2,1)S(1)}, bf16[128,512]{1,0:T(8,128)(2,1)S(1)}, u32[]{:S(2)}, u32[]{:S(2)}) %collective-permute-start.9) | collective-permute-done | bytes 131104 | tf_op jit(solution)/shard_map/ppermute | solution.py:193
  24.5 2.3 %layer_1_1.1.refs_1_ = bf16[128,512]{1,0:T(8,128)(2,1)S(1)} custom-call(bf16[128,512]{1,0:T(8,128)(2,1)S(1)} %collective-permute-done.9.refs_0_.refs_1_, bf16[128,512]{1,0:T(8,128)(2,1)S(1)} %collective-permute-done.9.refs_0_.refs_1_, bf16[128,512]{1,0:T(8,128)(2,1)S(1)} %layer_0_1.1.refs_2_, bf16[2,16,512]{2,1,0:T(8,128)(2,1)S(1)} %copy-done.5, ...), custom_call_target="tpu_custom_call" | custom-call | tf_op jit(solution)/shard_map/layer_1_1/pallas_call | solution.py:184
  26.9 0.0 copy-start.6
  26.9 1.3 %collective-permute-done.10.refs_0_.refs_1_ = bf16[128,512]{1,0:T(8,128)(2,1)S(1)} collective-permute-done((bf16[128,512]{1,0:T(8,128)(2,1)S(1)}, bf16[128,512]{1,0:T(8,128)(2,1)S(1)}, u32[]{:S(2)}, u32[]{:S(2)}) %collective-permute-start.10) | collective-permute-done | bytes 131104 | tf_op jit(solution)/shard_map/ppermute | solution.py:193
  28.2 2.3 %layer_1_2.1.refs_2_ = bf16[128,512]{1,0:T(8,128)(2,1)S(1)} custom-call(bf16[128,512]{1,0:T(8,128)(2,1)S(1)} %collective-permute-done.10.refs_0_.refs_1_, bf16[128,512]{1,0:T(8,128)(2,1)S(1)} %collective-permute-done.10.refs_0_.refs_1_, bf16[128,512]{1,0:T(8,128)(2,1)S(1)} %layer_0_2.1.refs_2_, bf16[2,16,512]{2,1,0:T(8,128)(2,1)S(1)} %copy-done.5, ...), custom_call_target="tpu_custom_call" | custom-call | tf_op jit(solution)/shard_map/layer_1_2/pallas_call | solution.py:184
  30.5 0.0 copy-done.6
  30.5 0.0 copy-start.7
  30.5 1.3 %collective-permute-done.8.refs_0_.refs_1_ = bf16[128,512]{1,0:T(8,128)(2,1)S(1)} collective-permute-done((bf16[128,512]{1,0:T(8,128)(2,1)S(1)}, bf16[128,512]{1,0:T(8,128)(2,1)S(1)}, u32[]{:S(2)}, u32[]{:S(2)}) %collective-permute-start.8) | collective-permute-done | bytes 131104 | tf_op jit(solution)/shard_map/ppermute | solution.py:193
  31.8 2.3 %layer_1_0.1.refs_0_ = bf16[128,512]{1,0:T(8,128)(2,1)S(1)} custom-call(bf16[128,512]{1,0:T(8,128)(2,1)S(1)} %collective-permute-done.8.refs_0_.refs_1_, bf16[128,512]{1,0:T(8,128)(2,1)S(1)} %collective-permute-done.8.refs_0_.refs_1_, bf16[128,512]{1,0:T(8,128)(2,1)S(1)} %layer_0_0.1.refs_2_, bf16[2,16,512]{2,1,0:T(8,128)(2,1)S(1)} %copy-done.5, ...), custom_call_target="tpu_custom_call" | custom-call | tf_op jit(solution)/shard_map/layer_1_0/pallas_call | solution.py:184
  34.2 0.0 copy-done.7
  34.2 0.0 copy-start.8
  34.2 1.0 %collective-permute-start.11 = (bf16[3,64,512]{2,1,0:T(8,128)(2,1)S(1)}, bf16[3,64,512]{2,1,0:T(8,128)(2,1)S(1)}, u32[]{:S(2)}, u32[]{:S(2)}) collective-permute-start(bf16[3,64,512]{2,1,0:T(8,128)(2,1)S(1)} %pad_maximum_fusion), channel_id=1, source_target_pairs={{0,1},{1,0},{2,3},{3,2},{4,5},{5,4},{6,7},{7,6},{8,9},{9,8},{10,11... | collective-permute-start | bytes 589832 | tf_op jit(solution)/shard_map/ppermute | solution.py:195
  35.2 1.1 %collective-permute-done.11.recv_ref = bf16[3,64,512]{2,1,0:T(8,128)(2,1)S(1)} collective-permute-done((bf16[3,64,512]{2,1,0:T(8,128)(2,1)S(1)}, bf16[3,64,512]{2,1,0:T(8,128)(2,1)S(1)}, u32[]{:S(2)}, u32[]{:S(2)}) %collective-permute-start.11) | collective-permute-done | bytes 196640 | tf_op jit(solution)/shard_map/ppermute | solution.py:195
  36.3 0.0 copy-done.8
  36.3 0.0 copy-start.11
  36.3 0.7 %copy-done.11 = bf16[3,64,512]{2,1,0:T(8,128)(2,1)} copy-done((bf16[3,64,512]{2,1,0:T(8,128)(2,1)}, bf16[3,64,512]{2,1,0:T(8,128)(2,1)S(1)}, u32[]{:S(2)}) %copy-start.11) | copy-done | bytes 196632
  37.0 2.0 %assemble.1 = bf16[3,32,4,512]{3,2,1,0:T(4,128)(2,1)} custom-call(bf16[3,64,512]{2,1,0:T(8,128)(2,1)} %copy-done.11, bf16[128,512]{1,0:T(8,128)(2,1)} %copy-done.8, bf16[128,512]{1,0:T(8,128)(2,1)} %copy-done.6, bf16[128,512]{1,0:T(8,128)(2,1)} %copy-done.7), custom_call_target="tpu_custom_call" | custom-call | tf_op jit(solution)/shard_map/assemble/pallas_call | solution.py:196
  (8 shorter events, 0.1 us)
Async XLA Ops:
  0.0 12.6 %copy-start.3 = (bf16[1,512,512]{2,1,0:T(8,128)(2,1)S(1)}, bf16[1,512,512]{2,1,0:T(8,128)(2,1)}, u32[]{:S(2)}) copy-start(bf16[1,512,512]{2,1,0:T(8,128)(2,1)} %refs_14_.11) | copy-start | bytes 1572868
  0.0 12.6 %copy-start.2 = (bf16[1,512,512]{2,1,0:T(8,128)(2,1)S(1)}, bf16[1,512,512]{2,1,0:T(8,128)(2,1)}, u32[]{:S(2)}) copy-start(bf16[1,512,512]{2,1,0:T(8,128)(2,1)} %refs_13_.11) | copy-start | bytes 1572868
  1.5 10.2 %collective-permute-start.4 = (bf16[2,16,512]{2,1,0:T(8,128)(2,1)}, bf16[2,16,512]{2,1,0:T(8,128)(2,1)S(1)}, u32[]{:S(2)}, u32[]{:S(2)}) collective-permute-start(bf16[2,16,512]{2,1,0:T(8,128)(2,1)} %prep_cache.1.refs_3_), channel_id=1, source_target_pairs={{0,1},{1,0},{2,3},{3,2},{4,5},{5,4},{6,7},{7,6},{8,9},{9,8},{10,11... | collective-permute-start | bytes 98312 | tf_op jit(solution)/shard_map/ppermute | solution.py:173
  2.2 7.4 %collective-permute-start.3 = (bf16[2,16,512]{2,1,0:T(8,128)(2,1)}, bf16[2,16,512]{2,1,0:T(8,128)(2,1)S(1)}, u32[]{:S(2)}, u32[]{:S(2)}) collective-permute-start(bf16[2,16,512]{2,1,0:T(8,128)(2,1)} %prep_cache.1.refs_3_), channel_id=1, source_target_pairs={{0,12},{4,0},{8,4},{12,8},{1,13},{5,1},{9,5},{13,9},{2,14},{6,2},{... | collective-permute-start | bytes 98312 | tf_op jit(solution)/shard_map/ppermute | solution.py:172
  5.5 4.2 %collective-permute-start.2 = (bf16[2,16,512]{2,1,0:T(8,128)(2,1)}, bf16[2,16,512]{2,1,0:T(8,128)(2,1)S(1)}, u32[]{:S(2)}, u32[]{:S(2)}) collective-permute-start(bf16[2,16,512]{2,1,0:T(8,128)(2,1)} %prep_cache.1.refs_3_), channel_id=1, source_target_pairs={{0,8},{4,12},{8,0},{12,4},{1,9},{5,13},{9,1},{13,5},{2,10},{6,14},... | collective-permute-start | bytes 98312 | tf_op jit(solution)/shard_map/ppermute | solution.py:172
  5.5 5.7 %collective-permute-start.1 = (bf16[2,16,512]{2,1,0:T(8,128)(2,1)}, bf16[2,16,512]{2,1,0:T(8,128)(2,1)S(1)}, u32[]{:S(2)}, u32[]{:S(2)}) collective-permute-start(bf16[2,16,512]{2,1,0:T(8,128)(2,1)} %prep_cache.1.refs_3_), channel_id=1, source_target_pairs={{0,4},{4,8},{8,12},{12,0},{1,5},{5,9},{9,13},{13,1},{2,6},{6,10},{... | collective-permute-start | bytes 98312 | tf_op jit(solution)/shard_map/ppermute | solution.py:172
  7.8 3.9 %collective-permute-start = (bf16[3,64,512]{2,1,0:T(8,128)(2,1)}, bf16[3,64,512]{2,1,0:T(8,128)(2,1)S(1)}, u32[]{:S(2)}, u32[]{:S(2)}) collective-permute-start(bf16[3,64,512]{2,1,0:T(8,128)(2,1)} %get-tuple-element.8), channel_id=1, source_target_pairs={{0,1},{1,0},{2,3},{3,2},{4,5},{5,4},{6,7},{7,6},{8,9},{9,8},{10,11... | collective-permute-start | bytes 589832 | tf_op jit(solution)/shard_map/ppermute | solution.py:160
  9.6 2.1 %collective-permute-start.7 = (bf16[2,16,512]{2,1,0:T(8,128)(2,1)S(1)}, bf16[2,16,512]{2,1,0:T(8,128)(2,1)S(1)}, u32[]{:S(2)}, u32[]{:S(2)}) collective-permute-start(bf16[2,16,512]{2,1,0:T(8,128)(2,1)S(1)} %collective-permute-done.3.refs_6_), channel_id=1, source_target_pairs={{0,1},{1,0},{2,3},{3,2},{4,5},{5,4},{6,7},{7,6},{8,9},{9,8},{10,11... | collective-permute-start | bytes 98312 | tf_op jit(solution)/shard_map/ppermute | solution.py:173
  9.7 2.3 %collective-permute-start.6 = (bf16[2,16,512]{2,1,0:T(8,128)(2,1)S(1)}, bf16[2,16,512]{2,1,0:T(8,128)(2,1)S(1)}, u32[]{:S(2)}, u32[]{:S(2)}) collective-permute-start(bf16[2,16,512]{2,1,0:T(8,128)(2,1)S(1)} %collective-permute-done.2.refs_5_), channel_id=1, source_target_pairs={{0,1},{1,0},{2,3},{3,2},{4,5},{5,4},{6,7},{7,6},{8,9},{9,8},{10,11... | collective-permute-start | bytes 98312 | tf_op jit(solution)/shard_map/ppermute | solution.py:173
  11.1 1.4 %collective-permute-start.5 = (bf16[2,16,512]{2,1,0:T(8,128)(2,1)S(1)}, bf16[2,16,512]{2,1,0:T(8,128)(2,1)S(1)}, u32[]{:S(2)}, u32[]{:S(2)}) collective-permute-start(bf16[2,16,512]{2,1,0:T(8,128)(2,1)S(1)} %collective-permute-done.1.refs_4_), channel_id=1, source_target_pairs={{0,1},{1,0},{2,3},{3,2},{4,5},{5,4},{6,7},{7,6},{8,9},{9,8},{10,11... | collective-permute-start | bytes 98312 | tf_op jit(solution)/shard_map/ppermute | solution.py:173
  12.6 1.4 %copy-start = (bf16[1,512,1536]{2,1,0:T(8,128)(2,1)S(1)}, bf16[1,512,1536]{2,1,0:T(8,128)(2,1)}, u32[]{:S(2)}) copy-start(bf16[1,512,1536]{2,1,0:T(8,128)(2,1)} %refs_12_.11) | copy-start | bytes 4718596
  14.0 1.0 %copy-start.4 = (bf16[1,512,512]{2,1,0:T(8,128)(2,1)S(1)}, bf16[1,512,512]{2,1,0:T(8,128)(2,1)}, u32[]{:S(2)}) copy-start(bf16[1,512,512]{2,1,0:T(8,128)(2,1)} %refs_15_.11) | copy-start | bytes 1572868
  15.0 0.8 %copy-start.5 = (bf16[2,16,512]{2,1,0:T(8,128)(2,1)S(1)}, bf16[2,16,512]{2,1,0:T(8,128)(2,1)}, u32[]{:S(2)}) copy-start(bf16[2,16,512]{2,1,0:T(8,128)(2,1)} %prep_cache.1.refs_3_) | copy-start | bytes 98308
  15.8 0.7 %copy-start.9 = (s32[8,8]{1,0:T(8,128)S(1)}, s32[8,8]{1,0:T(8,128)}, u32[]{:S(2)}) copy-start(s32[8,8]{1,0:T(8,128)} %refs_11_.11) | copy-start | bytes 772
  16.5 0.7 %copy-start.10 = (f32[1,2,512]{2,1,0:T(2,128)S(1)}, f32[1,2,512]{2,1,0:T(2,128)}, u32[]{:S(2)}) copy-start(f32[1,2,512]{2,1,0:T(2,128)} %refs_16_.11) | copy-start | bytes 12292
  17.1 1.4 %copy-start.1 = (bf16[1,512,1536]{2,1,0:T(8,128)(2,1)S(1)}, bf16[1,512,1536]{2,1,0:T(8,128)(2,1)}, u32[]{:S(2)}) copy-start(bf16[1,512,1536]{2,1,0:T(8,128)(2,1)} %refs_12_.11) | copy-start | bytes 4718596
  17.1 7.4 %collective-permute-start.9 = (bf16[128,512]{1,0:T(8,128)(2,1)S(1)}, bf16[128,512]{1,0:T(8,128)(2,1)S(1)}, u32[]{:S(2)}, u32[]{:S(2)}) collective-permute-start(bf16[128,512]{1,0:T(8,128)(2,1)S(1)} %layer_0_1.1.refs_2_), channel_id=1, source_target_pairs={{0,2},{1,3},{4,6},{5,7},{8,10},{9,11},{12,14},{13,15},{16,18},{17,... | collective-permute-start | bytes 393224 | tf_op jit(solution)/shard_map/ppermute | solution.py:193
  18.6 9.6 %collective-permute-start.10 = (bf16[128,512]{1,0:T(8,128)(2,1)S(1)}, bf16[128,512]{1,0:T(8,128)(2,1)S(1)}, u32[]{:S(2)}, u32[]{:S(2)}) collective-permute-start(bf16[128,512]{1,0:T(8,128)(2,1)S(1)} %layer_0_2.1.refs_2_), channel_id=1, source_target_pairs={{0,2},{1,3},{4,6},{5,7},{8,10},{9,11},{12,14},{13,15},{16,18},{17,... | collective-permute-start | bytes 393224 | tf_op jit(solution)/shard_map/ppermute | solution.py:193
  19.9 11.9 %collective-permute-start.8 = (bf16[128,512]{1,0:T(8,128)(2,1)S(1)}, bf16[128,512]{1,0:T(8,128)(2,1)S(1)}, u32[]{:S(2)}, u32[]{:S(2)}) collective-permute-start(bf16[128,512]{1,0:T(8,128)(2,1)S(1)} %layer_0_0.1.refs_2_), channel_id=1, source_target_pairs={{0,2},{1,3},{4,6},{5,7},{8,10},{9,11},{12,14},{13,15},{16,18},{17,... | collective-permute-start | bytes 393224 | tf_op jit(solution)/shard_map/ppermute | solution.py:193
  26.9 3.7 %copy-start.6 = (bf16[128,512]{1,0:T(8,128)(2,1)}, bf16[128,512]{1,0:T(8,128)(2,1)S(1)}, u32[]{:S(2)}) copy-start(bf16[128,512]{1,0:T(8,128)(2,1)S(1)} %layer_1_1.1.refs_1_) | copy-start | bytes 393220
  30.5 3.6 %copy-start.7 = (bf16[128,512]{1,0:T(8,128)(2,1)}, bf16[128,512]{1,0:T(8,128)(2,1)S(1)}, u32[]{:S(2)}) copy-start(bf16[128,512]{1,0:T(8,128)(2,1)S(1)} %layer_1_2.1.refs_2_) | copy-start | bytes 393220
  34.2 2.1 %copy-start.8 = (bf16[128,512]{1,0:T(8,128)(2,1)}, bf16[128,512]{1,0:T(8,128)(2,1)S(1)}, u32[]{:S(2)}) copy-start(bf16[128,512]{1,0:T(8,128)(2,1)S(1)} %layer_1_0.1.refs_0_) | copy-start | bytes 393220
  34.2 2.1 %collective-permute-start.11 = (bf16[3,64,512]{2,1,0:T(8,128)(2,1)S(1)}, bf16[3,64,512]{2,1,0:T(8,128)(2,1)S(1)}, u32[]{:S(2)}, u32[]{:S(2)}) collective-permute-start(bf16[3,64,512]{2,1,0:T(8,128)(2,1)S(1)} %pad_maximum_fusion), channel_id=1, source_target_pairs={{0,1},{1,0},{2,3},{3,2},{4,5},{5,4},{6,7},{7,6},{8,9},{9,8},{10,11... | collective-permute-start | bytes 589832 | tf_op jit(solution)/shard_map/ppermute | solution.py:195
  36.3 0.7 %copy-start.11 = (bf16[3,64,512]{2,1,0:T(8,128)(2,1)}, bf16[3,64,512]{2,1,0:T(8,128)(2,1)S(1)}, u32[]{:S(2)}) copy-start(bf16[3,64,512]{2,1,0:T(8,128)(2,1)S(1)} %collective-permute-done.11.recv_ref) | copy-start | bytes 589828

commit v2 on v0

v2 whole, which is shorter than its diff:
```python
import functools

import jax
import jax.numpy as jnp
from jax import lax
from jax.experimental import pallas as pl
from jax.experimental.pallas import tpu as pltpu
from jax.sharding import PartitionSpec as P

HEADS = 8
NEG = -1e30
VMEM = pltpu.MemorySpace.VMEM
GRANT = 12 * 1024 * 1024
LANES = 128


def whole():
    return pl.BlockSpec(memory_space=VMEM)


def call(kernel, outs, operands, name, scratch=(), flops=0, out_specs=None):
    return pl.pallas_call(
        kernel,
        out_shape=outs,
        in_specs=[whole()] * len(operands),
        out_specs=jax.tree.map(lambda _: whole(), outs) if out_specs is None else out_specs,
        scratch_shapes=scratch,
        name=name,
        compiler_params=pltpu.CompilerParams(vmem_limit_bytes=GRANT),
        cost_estimate=pl.CostEstimate(flops=flops, bytes_accessed=1 << 20, transcendentals=0),
    )(*operands)


def group_of(dim, own_count, group_dev, feat, shape):
    at = lax.broadcasted_iota(jnp.int32, shape, dim)
    side = jnp.where(at < own_count, feat, 1 - feat)
    return side * group_dev + lax.rem(at, group_dev)


def norm(x, gain):
    mean_sq = jnp.mean(x * x, axis=-1, keepdims=True)
    return x * lax.rsqrt(mean_sq + 1e-06) * gain


def low_lanes(tokens, head_dim):
    return lax.broadcasted_iota(jnp.int32, (tokens, LANES), 1) < head_dim


def attend(query, keys, values, bias, low):
    tokens, width = query.shape
    key_n = keys.shape[0]
    bias = jnp.concatenate([bias, bias], axis=0)
    ones = jnp.ones((key_n, LANES), jnp.bfloat16)
    zero = jnp.zeros((), jnp.bfloat16)
    outs = []
    for pair in range(width // LANES):
        span = slice(pair * LANES, (pair + 1) * LANES)
        q = query[:, span]
        stacked = jnp.concatenate([jnp.where(low, q, zero), jnp.where(low, zero, q)], axis=0)
        scores = lax.dot_general(stacked, keys[:, span], (((1,), (1,)), ((), ())), preferred_element_type=jnp.float32)
        scores = scores + bias
        expo = jnp.exp(scores - jnp.max(scores, axis=-1, keepdims=True)).astype(jnp.bfloat16)
        extended = jnp.concatenate([values[:, span], ones], axis=1)
        mixed = jnp.dot(expo, extended, preferred_element_type=jnp.float32)
        mixed = mixed[:, :LANES] / mixed[:, LANES:]
        outs.append(jnp.where(low, mixed[:tokens], mixed[tokens:]).astype(jnp.bfloat16))
    return jnp.concatenate(outs, axis=1)


def column_part(h, bias, wqkv, wout, wquery, gains):
    tokens, width = h.shape
    head_dim = width // HEADS
    scale = 1.0 / head_dim**0.5
    a = norm(h, gains[0, 0:1, :]).astype(jnp.bfloat16)
    qkv = jnp.dot(a, wqkv[0], preferred_element_type=jnp.float32)
    query = (qkv[:, :width].astype(jnp.bfloat16) * scale).astype(jnp.bfloat16)
    rest = qkv[:, width:].astype(jnp.bfloat16)
    mixed = attend(query, rest[:, :width], rest[:, width:], bias[...], low_lanes(tokens, head_dim))
    h1 = h + jnp.dot(mixed, wout[0], preferred_element_type=jnp.float32)
    b = norm(h1, gains[0, 1:2, :]).astype(jnp.bfloat16)
    item_q = jnp.dot(b, wquery[0], preferred_element_type=jnp.float32)
    return h1, (item_q.astype(jnp.bfloat16) * scale).astype(jnp.bfloat16)


def item_part(h1, item_q, near, far, bias, witem):
    tokens, width = h1.shape
    keys = jnp.concatenate([near[0], far[0]], axis=0)
    values = jnp.concatenate([near[1], far[1]], axis=0)
    item_mix = attend(item_q, keys, values, bias[...], low_lanes(tokens, width // HEADS))
    return (h1 + jnp.dot(item_mix, witem[0], preferred_element_type=jnp.float32)).astype(jnp.bfloat16)


def to_dense(wide, slabs, group_dev):
    for at, slab in enumerate(slabs):
        wide[at * group_dev:(at + 1) * group_dev, :] = slab.astype(jnp.float32)
    return wide[...].astype(jnp.bfloat16)


def load_kernel(count, x_hbm, cache_hbm, pattern_hbm, *refs):
    weights, outs = refs[:count], refs[count:2 * count]
    own_ref, cache_ref, feat_bias, item_bias, x_vmem, pattern, wide, sems = refs[2 * count:]
    micro, half, group_dev, _ = x_vmem.shape
    feat = lax.axis_index("feat")
    copies = [
        pltpu.make_async_copy(x_hbm.at[:, pl.ds(feat * half, half)], x_vmem, sems.at[0]),
        pltpu.make_async_copy(pattern_hbm, pattern, sems.at[1]),
        pltpu.make_async_copy(cache_hbm, cache_ref, sems.at[2]),
    ]
    for i, (src, dst) in enumerate(zip(weights, outs)):
        copies.append(pltpu.make_async_copy(src, dst, sems.at[3 + i]))
    for copy in copies:
        copy.start()
    copies[0].wait()
    for m in range(micro):
        own_ref[m] = to_dense(wide, [x_vmem[m, r] for r in range(half)], group_dev)
    tokens = feat_bias.shape[0]
    key_n = item_bias.shape[1]
    groups = 2 * group_dev
    copies[1].wait()
    shape = (tokens, groups)
    mine = group_of(0, tokens // 2, group_dev, feat, shape)
    one_hot = (mine == lax.broadcasted_iota(jnp.int32, shape, 1)).astype(jnp.float32)
    table = (pattern[...] != 0).astype(jnp.float32)
    spread = jnp.dot(one_hot, table, preferred_element_type=jnp.float32)
    full = lax.dot_general(spread, one_hot, (((1,), (1,)), ((), ())), preferred_element_type=jnp.float32)
    at_i = lax.broadcasted_iota(jnp.int32, (tokens, tokens), 0)
    at_j = lax.broadcasted_iota(jnp.int32, (tokens, tokens), 1)
    same_row = lax.rem(at_i, tokens // 2) // group_dev == lax.rem(at_j, tokens // 2) // group_dev
    feat_bias[...] = jnp.where((same_row & (full > 0.5)) | (at_i == at_j), 0.0, NEG)
    shape = (tokens, key_n)
    same = group_of(0, tokens // 2, group_dev, feat, shape) == group_of(1, key_n // 2, group_dev, feat, shape)
    item_bias[...] = jnp.where(same, 0.0, NEG)
    for copy in copies[2:]:
        copy.wait()


def enter_kernel(m, own_ref, other_ref, bias, wqkv, wout, wquery, gains, *refs):
    h1_ref, query_ref, wide = refs[-3:]
    _, test_n, group_dev, _ = other_ref.shape
    half = test_n // 2
    feat = lax.axis_index("feat")

    @pl.when(lax.axis_index("section") == 0)
    def _():
        theirs = to_dense(wide, [other_ref[m, feat * half + r] for r in range(half)], group_dev)
        h = jnp.concatenate([own_ref[m], theirs], axis=0).astype(jnp.float32)
        h1_ref[...], query_ref[...] = column_part(h, bias, wqkv, wout, wquery, gains)


def leave_kernel(h1_ref, query_ref, near, far, bias, witem, *refs):
    out_ref = refs[-1]

    @pl.when(lax.axis_index("section") == 0)
    def _():
        out_ref[...] = item_part(h1_ref[...], query_ref[...], near, far, bias, witem)


def layer_kernel(phase, h_ref, prev_ref, near, far, feat_bias, item_bias, wqkv, wout, wquery, witem, gains, out_ref):
    section = lax.axis_index("section")

    @pl.when(section == phase)
    def _():
        h1, query = column_part(h_ref[...].astype(jnp.float32), feat_bias, wqkv, wout, wquery, gains)
        out_ref[...] = item_part(h1, query, near, far, item_bias, witem)

    @pl.when(section != phase)
    def _():
        out_ref[...] = prev_ref[...]


def merge_kernel(count, *refs):
    pieces, out_ref, wide = refs[:count], refs[-2], refs[-1]
    _, _, rows, group_dev, _ = pieces[0].shape
    for kv in range(2):
        out_ref[kv] = to_dense(wide, [piece[0, kv, n] for piece in pieces for n in range(rows)], group_dev)


def from_dense(wide, value, put, group_dev):
    wide[...] = value.astype(jnp.float32)
    for r in range(wide.shape[0] // group_dev):
        put(r, wide[r * group_dev:(r + 1) * group_dev, :].astype(jnp.bfloat16))


def most_kernel(micro, *refs):
    own_refs, recv_refs = refs[:micro], refs[micro:2 * micro - 1]
    out_hbm, out, wide, sems = refs[-4:]
    _, test_n, group_dev, _ = out.shape
    half = test_n // 2
    feat = lax.axis_index("feat")
    copies = []
    for m in range(micro):
        parts = [(feat, own_refs[m][:half * group_dev])]
        if m + 1 < micro:
            parts.append((1 - feat, recv_refs[m][...]))
        for part, value in parts:
            def put(r, slab):
                out[m, part * half + r] = slab

            from_dense(wide, value, put, group_dev)
        where = m if m + 1 < micro else (m, pl.ds(feat * half, half))
        copies.append(pltpu.make_async_copy(out.at[where], out_hbm.at[where], sems.at[m]))
        copies[-1].start()
    for copy in copies:
        copy.wait()


def last_kernel(recv_ref, _, out_hbm, out, wide, sem):
    micro, test_n, group_dev, _ = out_hbm.shape
    half = test_n // 2

    def put(r, slab):
        out[r] = slab

    from_dense(wide, recv_ref[...], put, group_dev)
    start = (1 - lax.axis_index("feat")) * half
    copy = pltpu.make_async_copy(out, out_hbm.at[micro - 1, pl.ds(start, half)], sem)
    copy.start()
    copy.wait()


def per_device(test_rows, train_cache, pattern, feat_qkv, feat_out, item_query, item_out, gains):
    micro, test_n, group_dev, width = test_rows.shape
    sections = lax.axis_size("section")
    rows = lax.axis_size("rows")
    half = test_n // 2
    tokens = test_n * group_dev
    bf16, f32 = jnp.bfloat16, jnp.float32
    shaped = jax.ShapeDtypeStruct
    swap = [(0, 1), (1, 0)]
    other = lax.ppermute(test_rows, "feat", swap)
    pieces = []
    for shift in range(1, rows):
        pieces.append(lax.ppermute(train_cache, "rows", [(i, (i + shift) % rows) for i in range(rows)]))
    count = train_cache.shape[2] * group_dev * rows
    weights = (feat_qkv, feat_out, item_query, item_out, gains)
    *weights, own, cache, feat_bias, item_bias = pl.pallas_call(
        functools.partial(load_kernel, len(weights)),
        out_shape=[shaped(w.shape, w.dtype) for w in weights] + [
            shaped((micro, tokens // 2, width), bf16),
            shaped(train_cache.shape, bf16),
            shaped((tokens, tokens), f32),
            shaped((tokens, 2 * count), f32),
        ],
        in_specs=[pl.BlockSpec(memory_space=pltpu.MemorySpace.HBM)] * (3 + len(weights)),
        out_specs=[whole()] * (4 + len(weights)),
        scratch_shapes=[
            pltpu.VMEM((micro, half, group_dev, width), bf16),
            pltpu.VMEM(pattern.shape, pattern.dtype),
            pltpu.VMEM((tokens // 2, width), f32),
            pltpu.SemaphoreType.DMA((3 + len(weights),)),
        ],
        name="load",
        compiler_params=pltpu.CompilerParams(vmem_limit_bytes=GRANT),
    )(*[pltpu.with_memory_space_constraint(v, pltpu.MemorySpace.HBM) for v in (test_rows, train_cache, pattern, *weights)])
    wqkv, wout, wquery, witem, gains = weights
    dense = 2 * tokens * width * width
    block = shaped((tokens, width), bf16)

    def enter(m, *after):
        return call(
            functools.partial(enter_kernel, m), (shaped((tokens, width), f32), block),
            (own, other, feat_bias, wqkv, wout, wquery, gains, *after), f"enter_{m}",
            scratch=[pltpu.VMEM((tokens // 2, width), f32)], flops=5 * dense,
        )

    begun = [enter(0)]
    near = call(
        functools.partial(merge_kernel, rows), shaped((2, count, width), bf16), (cache, *pieces, begun[0][1]), "merge",
        scratch=[pltpu.VMEM((count, width), f32)],
    )
    far = lax.ppermute(near, "feat", swap)
    begun.append(enter(1, near))
    results, arriving = [], []
    for m in range(micro):
        if m >= len(begun):
            begun.append(enter(m, results[-1]))
        operands = (*begun[m], near, far, item_bias, witem, begun[-1][1])
        results.append(call(leave_kernel, block, operands, f"leave_{m}", flops=dense))
        arriving.append(lax.ppermute(results[m], "section", [(0, 1)]))
    for phase in range(1, sections):
        for m in range(micro):
            operands = (arriving[m], results[m], near, far, feat_bias, item_bias, wqkv, wout, wquery, witem, gains)
            results[m] = call(functools.partial(layer_kernel, phase), block, operands, f"layer_{phase}_{m}", flops=6 * dense)
            if phase + 1 < sections:
                arriving[m] = lax.ppermute(results[m], "section", [(phase, phase + 1)])
    received = [lax.ppermute(r[tokens // 2:], "feat", swap) for r in results]
    out_shape = shaped((micro, test_n, group_dev, width), bf16)
    hbm = pl.BlockSpec(memory_space=pl.ANY)
    out = call(
        functools.partial(most_kernel, micro), out_shape, (*results, *received[:-1]), "most", out_specs=hbm,
        scratch=[
            pltpu.VMEM(out_shape.shape, bf16), pltpu.VMEM((tokens // 2, width), f32), pltpu.SemaphoreType.DMA((micro,)),
        ],
    )
    out = pl.pallas_call(
        last_kernel,
        out_shape=out_shape,
        in_specs=[whole(), hbm],
        out_specs=hbm,
        input_output_aliases={1: 0},
        scratch_shapes=[
            pltpu.VMEM((half, group_dev, width), bf16), pltpu.VMEM((tokens // 2, width), f32), pltpu.SemaphoreType.DMA,
        ],
        name="last",
        compiler_params=pltpu.CompilerParams(vmem_limit_bytes=GRANT),
    )(received[-1], out)
    return out[None]


def solution(mesh):
    return jax.shard_map(
        per_device,
        mesh=mesh,
        in_specs=(
            P(None, ("groups", "rows"), "feat", None),
            P("section", None, ("groups", "rows"), "feat", None),
            P(),
            P("section", None, None),
            P("section", None, None),
            P("section", None, None),
            P("section", None, None),
            P("section", None, None),
        ),
        out_specs=P("section", None, ("groups", "rows"), "feat", None),
        check_vma=False,
    )
```

time: 149 us -> 28.7 us (0.19); the launches traced: 147 us -> 28.5 us
  local copies, waits for them, and re-layouts: 65.1 us -> 0.02 us
  matrix products: 41.6 us -> 0 us
  blocking collectives: 25.9 us -> 0 us
  Pallas kernels: 0 us -> 10.6 us
  starting transfers between devices: 3.86 us -> 12.4 us
  other arithmetic: 4.52 us -> 0 us
    dot_general x28 -> x0, matrix products: 31.9 us -> none  [the longest x4 7.14 us: per_device(): jnp.einsum('rhij,rjhd->rihd', weights, values, preferred_element_type=jnp...]
    reshape x28 -> x0, local copies, waits for them, and re-layouts: 31.2 us -> none  [the longest x4 7.3 us: per_device(): values = pairs[:, :, width:].reshape(test_n, groups, heads, head_dim)]
    all_gather x5 -> x0, blocking collectives: 25.9 us -> none  [the longest x4 15 us: per_device(): pairs = lax.all_gather(qkv[:, :, width:], 'feat', axis=1, tiled=True)]
    pallas_call x0 -> x13, Pallas kernels: none -> 10.6 us  [the longest x11 7.85 us: call(): pl.pallas_call(kernel, out_shape=outs, in_specs=[whole()] * len(operands)...]
    sub x4 -> x0, matrix products: 9.65 us -> none  [per_device(): weights = jax.nn.softmax(scores, axis=-1).astype(jnp.bfloat16)]
    slice x18 -> x3, local copies, waits for them, and re-layouts: 9.32 us -> 0.02 us  [per_device(): received = [lax.ppermute(r[tokens // 2:], 'feat', swap) for r in results]]
    ppermute x3 -> x11, starting transfers between devices: 3.86 us -> 12.4 us  [the longest x3 3.86 us: per_device(): arriving.append(lax.ppermute(results[m], 'section', [(0, 1)]))]
    dot_general x8 -> x0, local copies, waits for them, and re-layouts: 8.43 us -> none  [the longest x4 5.67 us: per_device(): term = jnp.dot(item_mix, witem, preferred_element_type=jnp.float32)]
  transfers between devices with their start and end apart: 3 -> 11, of which waited for: 3 -> 4; matrix products, arithmetic and copies ran while one was open for 7% -> 0% of each run, Pallas kernels for 0% -> 34%
where the time goes in v2:
time: 28.7 us; the launch traced here: 28.5 us
  starting transfers between devices  12.4 us (43%)
  Pallas kernels  10.6 us (37%)
  waiting for transfers between devices  5.38 us (19%)
    pallas_call x11, Pallas kernels, call(): pl.pallas_call(kernel, out_shape=outs, in_specs=[whole()] * len(operands)...  7.85 us
    ppermute x3, starting transfers between devices, per_device(): arriving.append(lax.ppermute(results[m], 'section', [(0, 1)]))  3.86 us
    ppermute x3, starting transfers between devices, per_device(): lax.ppermute(train_cache, 'rows', [(i, (i + shift) % rows) for i in range...  3.77 us
    ppermute x3, starting transfers between devices, per_device(): received = [lax.ppermute(r[tokens // 2:], 'feat', swap) for r in results]  2.69 us
    ppermute x3, waiting for transfers between devices, per_device(): arriving.append(lax.ppermute(results[m], 'section', [(0, 1)]))  2.62 us
    pallas_call x1, Pallas kernels, per_device(): pl.pallas_call(functools.partial(load_kernel, len(weights)), out_shape=[s...  2.04 us
    ppermute x3, waiting for transfers between devices, per_device(): lax.ppermute(train_cache, 'rows', [(i, (i + shift) % rows) for i in range...  1.67 us
    ppermute x1, starting transfers between devices, per_device(): far = lax.ppermute(near, 'feat', swap)  1.36 us
  transfers between devices with their start and end apart: 11, of which 4 were waited for; matrix products, arithmetic and copies ran while one was open for 0% of the time, Pallas kernels for 34%

profile of v2, /device:TPU:7, one launch (start us, length us, event | category | flops | bytes accessed | tf_op | source)
XLA Modules:
  0.0 28.5 jit_solution(10018750156818980170)
XLA Ops:
  0.0 0.7 %collective-permute-start = (bf16[3,32,4,512]{3,2,1,0:T(4,128)(2,1)}, bf16[3,32,4,512]{3,2,1,0:T(4,128)(2,1)S(1)}, u32[]{:S(2)}, u32[]{:S(2)}) collective-permute-start(bf16[3,32,4,512]{3,2,1,0:T(4,128)(2,1)} %x_hbm.1), channel_id=1, source_target_pairs={{0,1},{1,0},{2,3},{3,2},{4,5},{5,4},{6,7},{7,6},{8,9},{9,8},{10,11... | collective-permute-start | bytes 1179656 | tf_op jit(solution)/shard_map/ppermute | solution.py:230
  0.7 1.3 %collective-permute-start.1 = (bf16[1,2,4,4,512]{4,3,2,1,0:T(4,128)(2,1)}, bf16[1,2,4,4,512]{4,3,2,1,0:T(4,128)(2,1)S(1)}, u32[]{:S(2)}, u32[]{:S(2)}) collective-permute-start(bf16[1,2,4,4,512]{4,3,2,1,0:T(4,128)(2,1)} %cache_hbm.1), channel_id=1, source_target_pairs={{0,4},{4,8},{8,12},{12,0},{1,5},{5,9},{9,13},{13,1},{2,6},{6,10},{... | collective-permute-start | bytes 98312 | tf_op jit(solution)/shard_map/ppermute | solution.py:233
  2.0 2.0 %collective-permute-start.3 = (bf16[1,2,4,4,512]{4,3,2,1,0:T(4,128)(2,1)}, bf16[1,2,4,4,512]{4,3,2,1,0:T(4,128)(2,1)S(1)}, u32[]{:S(2)}, u32[]{:S(2)}) collective-permute-start(bf16[1,2,4,4,512]{4,3,2,1,0:T(4,128)(2,1)} %cache_hbm.1), channel_id=1, source_target_pairs={{0,12},{4,0},{8,4},{12,8},{1,13},{5,1},{9,5},{13,9},{2,14},{6,2},{... | collective-permute-start | bytes 98312 | tf_op jit(solution)/shard_map/ppermute | solution.py:233
  4.0 0.5 %collective-permute-start.2 = (bf16[1,2,4,4,512]{4,3,2,1,0:T(4,128)(2,1)}, bf16[1,2,4,4,512]{4,3,2,1,0:T(4,128)(2,1)S(1)}, u32[]{:S(2)}, u32[]{:S(2)}) collective-permute-start(bf16[1,2,4,4,512]{4,3,2,1,0:T(4,128)(2,1)} %cache_hbm.1), channel_id=1, source_target_pairs={{0,8},{4,12},{8,0},{12,4},{1,9},{5,13},{9,1},{13,5},{2,10},{6,14},... | collective-permute-start | bytes 98312 | tf_op jit(solution)/shard_map/ppermute | solution.py:233
  4.5 2.0 %load.1 = (bf16[1,512,1536]{2,1,0:T(8,128)(2,1)S(1)}, bf16[1,512,512]{2,1,0:T(8,128)(2,1)S(1)}, bf16[1,512,512]{2,1,0:T(8,128)(2,1)S(1)}, bf16[1,512,512]{2,1,0:...) custom-call(bf16[3,32,4,512]{3,2,1,0:T(4,128)(2,1)} %x_hbm.1, ...), custom_call_target="tpu_custom_call" | custom-call | tf_op jit(solution)/shard_map/load/pallas_call | solution.py:236
  6.5 0.0 collective-permute-done.other_ref
  6.5 0.0 collective-permute-done.1.refs_1_
  6.6 0.0 collective-permute-done.3.refs_3_
  6.6 1.7 %collective-permute-done.2.refs_2_ = bf16[1,2,4,4,512]{4,3,2,1,0:T(4,128)(2,1)S(1)} collective-permute-done((bf16[1,2,4,4,512]{4,3,2,1,0:T(4,128)(2,1)}, bf16[1,2,4,4,512]{4,3,2,1,0:T(4,128)(2,1)S(1)}, u32[]{:S(2)}, u32[]{:S(2)}) %collective-permute-start.2) | collective-permute-done | bytes 32800 | tf_op jit(solution)/shard_map/ppermute | solution.py:233
  8.2 0.1 merge.1.refs_0_.near
  8.3 1.4 %collective-permute-start.4 = (bf16[2,64,512]{2,1,0:T(8,128)(2,1)S(1)}, bf16[2,64,512]{2,1,0:T(8,128)(2,1)S(1)}, u32[]{:S(2)}, u32[]{:S(2)}) collective-permute-start(bf16[2,64,512]{2,1,0:T(8,128)(2,1)S(1)} %merge.1.refs_0_.near), channel_id=1, source_target_pairs={{0,1},{1,0},{2,3},{3,2},{4,5},{5,4},{6,7},{7,6},{8,9},{9,8},{10,11... | collective-permute-start | bytes 393224 | tf_op jit(solution)/shard_map/ppermute | solution.py:271
  9.7 1.0 %collective-permute-done.4.far = bf16[2,64,512]{2,1,0:T(8,128)(2,1)S(1)} collective-permute-done((bf16[2,64,512]{2,1,0:T(8,128)(2,1)S(1)}, bf16[2,64,512]{2,1,0:T(8,128)(2,1)S(1)}, u32[]{:S(2)}, u32[]{:S(2)}) %collective-permute-start.4) | collective-permute-done | bytes 131104 | tf_op jit(solution)/shard_map/ppermute | solution.py:271
  10.6 1.3 %collective-permute-start.8 = (bf16[128,512]{1,0:T(8,128)(2,1)S(1)}, bf16[128,512]{1,0:T(8,128)(2,1)S(1)}, u32[]{:S(2)}, u32[]{:S(2)}) collective-permute-start(bf16[128,512]{1,0:T(8,128)(2,1)S(1)} %leave_1.1.refs_0_.prev_ref), channel_id=1, source_target_pairs={{0,2},{1,3},{4,6},{5,7},{8,10},{9,11},{12,14},{13,15},{16,18},{17,... | collective-permute-start | bytes 393224 | tf_op jit(solution)/shard_map/ppermute | solution.py:279
  12.0 1.3 %collective-permute-start.7 = (bf16[128,512]{1,0:T(8,128)(2,1)S(1)}, bf16[128,512]{1,0:T(8,128)(2,1)S(1)}, u32[]{:S(2)}, u32[]{:S(2)}) collective-permute-start(bf16[128,512]{1,0:T(8,128)(2,1)S(1)} %leave_0.1.prev_ref), channel_id=1, source_target_pairs={{0,2},{1,3},{4,6},{5,7},{8,10},{9,11},{12,14},{13,15},{16,18},{17,... | collective-permute-start | bytes 393224 | tf_op jit(solution)/shard_map/ppermute | solution.py:279
  13.3 1.3 %collective-permute-start.5 = (bf16[128,512]{1,0:T(8,128)(2,1)S(1)}, bf16[128,512]{1,0:T(8,128)(2,1)S(1)}, u32[]{:S(2)}, u32[]{:S(2)}) collective-permute-start(bf16[128,512]{1,0:T(8,128)(2,1)S(1)} %leave_2.1.prev_ref), channel_id=1, source_target_pairs={{0,2},{1,3},{4,6},{5,7},{8,10},{9,11},{12,14},{13,15},{16,18},{17,... | collective-permute-start | bytes 393224 | tf_op jit(solution)/shard_map/ppermute | solution.py:279
  14.6 2.6 %collective-permute-done.8.h_ref = bf16[128,512]{1,0:T(8,128)(2,1)S(1)} collective-permute-done((bf16[128,512]{1,0:T(8,128)(2,1)S(1)}, bf16[128,512]{1,0:T(8,128)(2,1)S(1)}, u32[]{:S(2)}, u32[]{:S(2)}) %collective-permute-start.8) | collective-permute-done | bytes 131104 | tf_op jit(solution)/shard_map/ppermute | solution.py:279
  17.2 2.3 %layer_1_1.1.refs_1_ = bf16[128,512]{1,0:T(8,128)(2,1)S(1)} custom-call(bf16[128,512]{1,0:T(8,128)(2,1)S(1)} %collective-permute-done.8.h_ref, bf16[128,512]{1,0:T(8,128)(2,1)S(1)} %leave_1.1.refs_0_.prev_ref, bf16[2,64,512]{2,1,0:T(8,128)(2,1)S(1)} %merge.1.refs_0_.near, bf16[2,64,512]{2,1,0:T(8,128)(2,1)S(1)} %collective-permute-done.4.far, ...), custom_call_target="tpu_custom_call" | custom-call | flops 402653184 | bytes 1048576 | tf_op jit(solution)/shard_map/layer_1_1/pallas_call | solution.py:22
  19.6 1.8 %collective-permute-start.10 = (bf16[64,512]{1,0:T(8,128)(2,1)S(1)}, bf16[64,512]{1,0:T(8,128)(2,1)S(1)}, u32[]{:S(2)}, u32[]{:S(2)}) collective-permute-start(bf16[64,512]{1,0:T(8,128)(2,1)S(1)} %slice.14), channel_id=1, source_target_pairs={{0,1},{1,0},{2,3},{3,2},{4,5},{5,4},{6,7},{7,6},{8,9},{9,8},{10,11... | collective-permute-start | bytes 196616 | tf_op jit(solution)/shard_map/ppermute | solution.py:286
  21.4 0.0 collective-permute-done.7.h_ref
  21.4 2.3 %layer_1_0.1.refs_0_ = bf16[128,512]{1,0:T(8,128)(2,1)S(1)} custom-call(bf16[128,512]{1,0:T(8,128)(2,1)S(1)} %collective-permute-done.7.h_ref, bf16[128,512]{1,0:T(8,128)(2,1)S(1)} %leave_0.1.prev_ref, bf16[2,64,512]{2,1,0:T(8,128)(2,1)S(1)} %merge.1.refs_0_.near, bf16[2,64,512]{2,1,0:T(8,128)(2,1)S(1)} %collective-permute-done.4.far, ...), custom_call_target="tpu_custom_call" | custom-call | flops 402653184 | bytes 1048576 | tf_op jit(solution)/shard_map/layer_1_0/pallas_call | solution.py:22
  23.7 0.1 collective-permute-start.9
  23.8 0.0 collective-permute-done.5.h_ref
  23.8 2.3 %layer_1_2.1.refs_2_ = bf16[128,512]{1,0:T(8,128)(2,1)S(1)} custom-call(bf16[128,512]{1,0:T(8,128)(2,1)S(1)} %collective-permute-done.5.h_ref, bf16[128,512]{1,0:T(8,128)(2,1)S(1)} %leave_2.1.prev_ref, bf16[2,64,512]{2,1,0:T(8,128)(2,1)S(1)} %merge.1.refs_0_.near, bf16[2,64,512]{2,1,0:T(8,128)(2,1)S(1)} %collective-permute-done.4.far, ...), custom_call_target="tpu_custom_call" | custom-call | flops 402653184 | bytes 1048576 | tf_op jit(solution)/shard_map/layer_1_2/pallas_call | solution.py:22
  26.1 0.8 %collective-permute-start.6 = (bf16[64,512]{1,0:T(8,128)(2,1)S(1)}, bf16[64,512]{1,0:T(8,128)(2,1)S(1)}, u32[]{:S(2)}, u32[]{:S(2)}) collective-permute-start(bf16[64,512]{1,0:T(8,128)(2,1)S(1)} %slice.12), channel_id=1, source_target_pairs={{0,1},{1,0},{2,3},{3,2},{4,5},{5,4},{6,7},{7,6},{8,9},{9,8},{10,11... | collective-permute-start | bytes 196616 | tf_op jit(solution)/shard_map/ppermute | solution.py:286
  26.9 0.0 collective-permute-done.10.refs_4_
  26.9 0.0 collective-permute-done.9.refs_3_
  26.9 0.8 %most.1._ = bf16[3,32,4,512]{3,2,1,0:T(4,128)(2,1)} custom-call(bf16[128,512]{1,0:T(8,128)(2,1)S(1)} %layer_1_0.1.refs_0_, bf16[128,512]{1,0:T(8,128)(2,1)S(1)} %layer_1_1.1.refs_1_, bf16[128,512]{1,0:T(8,128)(2,1)S(1)} %layer_1_2.1.refs_2_, bf16[64,512]{1,0:T(8,128)(2,1)S(1)} %collective-permute-done.9.refs_3_, ...), custom_call_target="tpu_custom_call" | custom-call | bytes 1048576 | tf_op jit(solution)/shard_map/most/pallas_call | solution.py:22
  27.7 0.1 collective-permute-done.6.recv_ref
  27.8 0.7 %last.1 = bf16[3,32,4,512]{3,2,1,0:T(4,128)(2,1)} custom-call(bf16[64,512]{1,0:T(8,128)(2,1)S(1)} %collective-permute-done.6.recv_ref, bf16[3,32,4,512]{3,2,1,0:T(4,128)(2,1)} %most.1._), custom_call_target="tpu_custom_call", output_to_operand_aliasing={{}: (1, {})} | custom-call | tf_op jit(solution)/shard_map/last/pallas_call | solution.py:295
  (9 shorter events, 0.1 us)
Async XLA Ops:
  0.0 6.5 %collective-permute-start = (bf16[3,32,4,512]{3,2,1,0:T(4,128)(2,1)}, bf16[3,32,4,512]{3,2,1,0:T(4,128)(2,1)S(1)}, u32[]{:S(2)}, u32[]{:S(2)}) collective-permute-start(bf16[3,32,4,512]{3,2,1,0:T(4,128)(2,1)} %x_hbm.1), channel_id=1, source_target_pairs={{0,1},{1,0},{2,3},{3,2},{4,5},{5,4},{6,7},{7,6},{8,9},{9,8},{10,11... | collective-permute-start | bytes 1179656 | tf_op jit(solution)/shard_map/ppermute | solution.py:230
  0.7 5.9 %collective-permute-start.1 = (bf16[1,2,4,4,512]{4,3,2,1,0:T(4,128)(2,1)}, bf16[1,2,4,4,512]{4,3,2,1,0:T(4,128)(2,1)S(1)}, u32[]{:S(2)}, u32[]{:S(2)}) collective-permute-start(bf16[1,2,4,4,512]{4,3,2,1,0:T(4,128)(2,1)} %cache_hbm.1), channel_id=1, source_target_pairs={{0,4},{4,8},{8,12},{12,0},{1,5},{5,9},{9,13},{13,1},{2,6},{6,10},{... | collective-permute-start | bytes 98312 | tf_op jit(solution)/shard_map/ppermute | solution.py:233
  2.0 4.6 %collective-permute-start.3 = (bf16[1,2,4,4,512]{4,3,2,1,0:T(4,128)(2,1)}, bf16[1,2,4,4,512]{4,3,2,1,0:T(4,128)(2,1)S(1)}, u32[]{:S(2)}, u32[]{:S(2)}) collective-permute-start(bf16[1,2,4,4,512]{4,3,2,1,0:T(4,128)(2,1)} %cache_hbm.1), channel_id=1, source_target_pairs={{0,12},{4,0},{8,4},{12,8},{1,13},{5,1},{9,5},{13,9},{2,14},{6,2},{... | collective-permute-start | bytes 98312 | tf_op jit(solution)/shard_map/ppermute | solution.py:233
  4.0 4.2 %collective-permute-start.2 = (bf16[1,2,4,4,512]{4,3,2,1,0:T(4,128)(2,1)}, bf16[1,2,4,4,512]{4,3,2,1,0:T(4,128)(2,1)S(1)}, u32[]{:S(2)}, u32[]{:S(2)}) collective-permute-start(bf16[1,2,4,4,512]{4,3,2,1,0:T(4,128)(2,1)} %cache_hbm.1), channel_id=1, source_target_pairs={{0,8},{4,12},{8,0},{12,4},{1,9},{5,13},{9,1},{13,5},{2,10},{6,14},... | collective-permute-start | bytes 98312 | tf_op jit(solution)/shard_map/ppermute | solution.py:233
  8.3 2.3 %collective-permute-start.4 = (bf16[2,64,512]{2,1,0:T(8,128)(2,1)S(1)}, bf16[2,64,512]{2,1,0:T(8,128)(2,1)S(1)}, u32[]{:S(2)}, u32[]{:S(2)}) collective-permute-start(bf16[2,64,512]{2,1,0:T(8,128)(2,1)S(1)} %merge.1.refs_0_.near), channel_id=1, source_target_pairs={{0,1},{1,0},{2,3},{3,2},{4,5},{5,4},{6,7},{7,6},{8,9},{9,8},{10,11... | collective-permute-start | bytes 393224 | tf_op jit(solution)/shard_map/ppermute | solution.py:271
  10.6 6.6 %collective-permute-start.8 = (bf16[128,512]{1,0:T(8,128)(2,1)S(1)}, bf16[128,512]{1,0:T(8,128)(2,1)S(1)}, u32[]{:S(2)}, u32[]{:S(2)}) collective-permute-start(bf16[128,512]{1,0:T(8,128)(2,1)S(1)} %leave_1.1.refs_0_.prev_ref), channel_id=1, source_target_pairs={{0,2},{1,3},{4,6},{5,7},{8,10},{9,11},{12,14},{13,15},{16,18},{17,... | collective-permute-start | bytes 393224 | tf_op jit(solution)/shard_map/ppermute | solution.py:279
  12.0 9.4 %collective-permute-start.7 = (bf16[128,512]{1,0:T(8,128)(2,1)S(1)}, bf16[128,512]{1,0:T(8,128)(2,1)S(1)}, u32[]{:S(2)}, u32[]{:S(2)}) collective-permute-start(bf16[128,512]{1,0:T(8,128)(2,1)S(1)} %leave_0.1.prev_ref), channel_id=1, source_target_pairs={{0,2},{1,3},{4,6},{5,7},{8,10},{9,11},{12,14},{13,15},{16,18},{17,... | collective-permute-start | bytes 393224 | tf_op jit(solution)/shard_map/ppermute | solution.py:279
  13.3 10.5 %collective-permute-start.5 = (bf16[128,512]{1,0:T(8,128)(2,1)S(1)}, bf16[128,512]{1,0:T(8,128)(2,1)S(1)}, u32[]{:S(2)}, u32[]{:S(2)}) collective-permute-start(bf16[128,512]{1,0:T(8,128)(2,1)S(1)} %leave_2.1.prev_ref), channel_id=1, source_target_pairs={{0,2},{1,3},{4,6},{5,7},{8,10},{9,11},{12,14},{13,15},{16,18},{17,... | collective-permute-start | bytes 393224 | tf_op jit(solution)/shard_map/ppermute | solution.py:279
  19.6 7.4 %collective-permute-start.10 = (bf16[64,512]{1,0:T(8,128)(2,1)S(1)}, bf16[64,512]{1,0:T(8,128)(2,1)S(1)}, u32[]{:S(2)}, u32[]{:S(2)}) collective-permute-start(bf16[64,512]{1,0:T(8,128)(2,1)S(1)} %slice.14), channel_id=1, source_target_pairs={{0,1},{1,0},{2,3},{3,2},{4,5},{5,4},{6,7},{7,6},{8,9},{9,8},{10,11... | collective-permute-start | bytes 196616 | tf_op jit(solution)/shard_map/ppermute | solution.py:286
  23.7 3.2 %collective-permute-start.9 = (bf16[64,512]{1,0:T(8,128)(2,1)S(1)}, bf16[64,512]{1,0:T(8,128)(2,1)S(1)}, u32[]{:S(2)}, u32[]{:S(2)}) collective-permute-start(bf16[64,512]{1,0:T(8,128)(2,1)S(1)} %slice.13), channel_id=1, source_target_pairs={{0,1},{1,0},{2,3},{3,2},{4,5},{5,4},{6,7},{7,6},{8,9},{9,8},{10,11... | collective-permute-start | bytes 196616 | tf_op jit(solution)/shard_map/ppermute | solution.py:286
  26.1 1.7 %collective-permute-start.6 = (bf16[64,512]{1,0:T(8,128)(2,1)S(1)}, bf16[64,512]{1,0:T(8,128)(2,1)S(1)}, u32[]{:S(2)}, u32[]{:S(2)}) collective-permute-start(bf16[64,512]{1,0:T(8,128)(2,1)S(1)} %slice.12), channel_id=1, source_target_pairs={{0,1},{1,0},{2,3},{3,2},{4,5},{5,4},{6,7},{7,6},{8,9},{9,8},{10,11... | collective-permute-start | bytes 196616 | tf_op jit(solution)/shard_map/ppermute | solution.py:286
